TPU v7x, 128 devices: a whole 4x4x4 slice. The times are simulated.
128 devices in a mesh: sx: 4 (over y_hi, core), sy: 16 (over z, x), depth: 2 (over y_lo).
Axes of the slice: x: 4, y: 4 (y_hi: 2, y_lo: 2; y = y_hi * 2 + y_lo), z: 4, core: 2. Of those that a mesh axis runs over, the one named last changes fastest.
Arguments:
- probe_wave: float32 [2, 128, 128], replicated, may hold values from -4.2 to 4.2
- transmission: float32 [2, 8, 512, 4096], P(None, 'depth', 'sx', 'sy'), may hold values from -0.6 to 0.6
- scan_offsets: int32 [4, 16, 4, 2], P('sx', 'sy'), may hold values from -64 to 192, as said below
- pattern_shifts: int32 [4, 16, 4, 2], P('sx', 'sy'), may hold values from -8 to 8
- patterns: float32 [4, 16, 4, 128, 128], P('sx', 'sy'), may hold values from 0 to 9
Outputs:
- transmission_grad: float32 [2, 8, 512, 4096], P(None, 'depth', 'sx', 'sy')
- probe_grad: float32 [2, 128, 128], replicated
- mean_error: float32 [], replicated
Inputs may be any that keep to these rules, and one draw needn't show every extreme that they name: `scan_offsets`: row offsets lie from -64 to 64 and column offsets from -64 to 192; on every scan tile some position takes the smallest and some the largest value of each.
All inputs are finite; a program needn't handle non-finite values.
Results may differ from a plain program's by a relative error of at most 0.0003.
Values sent between devices are 32-bit elements; how exact they have to be, the bound alone decides.
No kernel may reach another device: no remote copies, remote signals or barrier semaphores. Data moves between devices by JAX's collectives and lax.ppermute only.
A program may use at most 64 MiB of HBM per device.

v0:
```python
import functools

import jax
import jax.numpy as jnp
import numpy as np
from jax import lax
from jax.experimental import pallas as pl
from jax.experimental.pallas import tpu as pltpu
from jax.sharding import PartitionSpec as P


FRESNEL = 12.0
WIN = 128
HALF = 64
TALL = WIN + 8
F32 = jnp.float32
BF16 = jnp.bfloat16
VMEM_LIMIT = 16 * 1024 * 1024


def tables():
    n = np.arange(WIN)
    fourier = np.exp(-2j * np.pi * (np.outer(n, n) % WIN) / WIN) / np.sqrt(WIN)
    freq = np.where(n < WIN // 2, n, n - WIN) / WIN
    phase = np.exp(-1j * FRESNEL * freq * freq)
    prop = fourier.conj() @ (phase[:, None] * fourier)
    exit_left = fourier @ prop
    exit_right = prop @ fourier
    return prop, exit_left, exit_right


def right_block(m):
    return np.block([[m.real, m.imag], [-m.imag, m.real]])


def left_block(m):
    return np.block([[m.real, -m.imag], [m.imag, m.real]])


def halves(m):
    m = m.astype(np.float32)
    hi = m.astype(jnp.bfloat16)
    lo = (m - hi.astype(np.float32)).astype(jnp.bfloat16)
    return np.stack([hi, lo])


def constants():
    prop, exit_left, exit_right = tables()
    steps = np.stack([halves(right_block(prop)), halves(left_block(prop))])
    exits = np.stack([halves(right_block(exit_right)), halves(left_block(exit_left))])
    return jnp.asarray(steps), jnp.asarray(exits)


def split(x):
    hi = x.astype(BF16)
    return hi, (x - hi.astype(F32)).astype(BF16)


def mm(a, b):
    return jnp.dot(a, b, preferred_element_type=F32)


def mm3(a, b):
    return mm(a[0], b[0]) + (mm(a[1], b[0]) + mm(a[0], b[1]))


def apply_both(fields, right, left):
    rows = jnp.concatenate([jnp.concatenate([re, im], axis=1) for re, im in fields], axis=0)
    z = mm3(split(rows), right)
    cols = jnp.concatenate(
        [
            jnp.concatenate([z[p * WIN : (p + 1) * WIN, :WIN], z[p * WIN : (p + 1) * WIN, WIN:]], axis=0)
            for p in range(len(fields))
        ],
        axis=1,
    )
    y = mm3(left, split(cols))
    return [
        (y[:WIN, p * WIN : (p + 1) * WIN], y[WIN:, p * WIN : (p + 1) * WIN]) for p in range(len(fields))
    ]


def times(a, b):
    return a[0] * b[0] - a[1] * b[1], a[0] * b[1] + a[1] * b[0]


def conj_times(a, b):
    return a[0] * b[0] + a[1] * b[1], a[0] * b[1] - a[1] * b[0]


def pair(ref, i):
    return ref[i, 0], ref[i, 1]


def roll_half(x):
    return pltpu.roll(x, HALF, axis=x.ndim - 1)


def join(low, high):
    lane = lax.broadcasted_iota(jnp.int32, low.shape, low.ndim - 1)
    return jnp.where(lane < HALF, low, high)


def fetch(src, dst, sem):
    copy = pltpu.make_async_copy(src, dst, sem)
    copy.start()
    return copy


def pack_kernel(pos, source, col1, col2, row1, row2, tile, sems):
    fetch(source, tile, sems.at[0]).wait()
    right = join(roll_half(tile[0, :, :, 128:]), tile[1, :, :, 128:])
    left = join(tile[0, :, :, :128], roll_half(tile[1, :, :, :128]))
    even = pos[1] == 0

    @pl.when(even)
    def _():
        col1[...] = right
        col2[...] = left

    @pl.when(jnp.logical_not(even))
    def _():
        col1[...] = left
        col2[...] = right

    low = pos[2] * 64
    row1[...] = tile[:, :, pl.ds(pl.multiple_of(64 - low, 64), 64), :]
    row2[...] = tile[:, :, pl.ds(pl.multiple_of(low, 64), 64), :]


def pack_corners_kernel(pos, col1, col2, first, second):
    even = pos[1] == 0
    low = pos[2] * 64
    for out, start in ((first, 64 - low), (second, low)):
        rows = pl.ds(pl.multiple_of(start, 64), 64)

        @pl.when(even)
        def _():
            out[:, :, :128] = col2[:, rows, :]
            out[:, :, 128:] = col1[:, rows, :]

        @pl.when(jnp.logical_not(even))
        def _():
            out[:, :, :128] = col1[:, rows, :]
            out[:, :, 128:] = col2[:, rows, :]


def load_window(ext, c, k, row, block, shift):
    base = pl.multiple_of(row // 8 * 8, 8)
    wide = ext[c, k, pl.ds(base, TALL), pl.ds(pl.multiple_of(block * 128, 128), 256)]
    wide = pltpu.roll(wide, (256 - shift) & 255, axis=1)[:, :WIN]
    return pltpu.roll(wide, (TALL - row % 8) % TALL, axis=0)[:WIN]


def place(pos, p):
    row = pos[3 + 2 * p] + HALF
    col = pos[4 + 2 * p] + 128
    return row, col // 128, col % 128


def forward_kernel(
    count, pos, probe_h, tile, col1_h, col2_h, row1, row2, crn1_h, crn2_h, mats_h,
    wave, win, psi_h, ext, probe, mats, psi, cols, corners, sems,
):
    slabs = tile.shape[1]
    odd_row = pos[2]
    starts = (pl.multiple_of(192 * (1 - odd_row), 64), pl.multiple_of(192 * odd_row, 64))
    first = pos[1]
    near = [
        fetch(col1_h, cols.at[1 - first], sems.at[0]),
        fetch(col2_h, cols.at[first], sems.at[1]),
        fetch(crn1_h, corners.at[0], sems.at[2]),
        fetch(crn2_h, corners.at[1], sems.at[3]),
    ]
    far = [
        fetch(tile, ext.at[:, :, pl.ds(64, 128), pl.ds(128, 256)], sems.at[4]),
        fetch(row1, ext.at[:, :, pl.ds(starts[0], 64), pl.ds(128, 256)], sems.at[5]),
        fetch(row2, ext.at[:, :, pl.ds(starts[1], 64), pl.ds(128, 256)], sems.at[6]),
    ]
    loads = [fetch(probe_h, probe, sems.at[7]), fetch(mats_h, mats, sems.at[8])]
    for copy in near:
        copy.wait()

    def sides(rows, left, right):
        ext[0, :, rows, 0:128] = roll_half(left)
        ext[1, :, rows, 0:128] = left
        ext[0, :, rows, 384:512] = right
        ext[1, :, rows, 384:512] = roll_half(right)

    sides(slice(64, 192), cols[0], cols[1])
    for i in range(2):
        sides(pl.ds(starts[i], 64), corners[i, :, :, :128], corners[i, :, :, 128:])
    for copy in far:
        copy.wait()
    for copy in loads:
        copy.wait()
    for p in range(count):
        row, block, shift = place(pos, p)
        for k in range(slabs):
            win[k, p, 0] = load_window(ext, 0, k, row, block, shift) + 1.0
            win[k, p, 1] = load_window(ext, 1, k, row, block, shift)

    @pl.when(pos[0] == 0)
    def _():
        right = (mats[0, 0], mats[0, 1])
        left = (mats[1, 0], mats[1, 1])
        fields = [(probe[0], probe[1])] * count
        saves = []
        for k in range(slabs):
            if k:
                for p in range(count):
                    psi[k - 1, p, 0], psi[k - 1, p, 1] = fields[p]
                saves.append(fetch(psi.at[k - 1], psi_h.at[k - 1], sems.at[8 + k]))
            fields = apply_both([times(fields[p], pair(win.at[k], p)) for p in range(count)], right, left)
        for p in range(count):
            wave[p, 0], wave[p, 1] = fields[p]
        for copy in saves:
            copy.wait()


def add_window(ext, c, k, row, block, shift, piece):
    tall = pltpu.roll(jnp.concatenate([piece, jnp.zeros((TALL - WIN, WIN), F32)], axis=0), row % 8, axis=0)
    wide = pltpu.roll(jnp.concatenate([tall, jnp.zeros_like(tall)], axis=1), shift, axis=1)
    base = pl.multiple_of(row // 8 * 8, 8)
    at = (c, k, pl.ds(base, TALL), pl.ds(pl.multiple_of(block * 128, 128), 256))
    ext[at] = ext[at] + wide


def strips(ext, rows):
    left = join(roll_half(ext[0, :, rows, 0:128]), ext[1, :, rows, 0:128])
    right = join(ext[0, :, rows, 384:512], roll_half(ext[1, :, rows, 384:512]))
    return left, right


def emit_rims(pos, ext, first, second):
    def rim(out, start):
        rows = pl.ds(pl.multiple_of(start, 64), 64)
        out[:, :, 0:256] = ext[0, :, rows, 128:384]
        out[:, :, 256:512] = ext[1, :, rows, 128:384]
        out[:, :, 512:640], out[:, :, 640:768] = strips(ext, rows)

    odd_row = pos[2]
    rim(first, 192 * (1 - odd_row))
    rim(second, 192 * odd_row)


def backward_slabs(count, pos, grads, win, incident, ext, right, left, ext_h, sems):
    slabs = win.shape[0]
    saves = []
    for k in reversed(range(slabs)):
        if grads[0] == "exit":
            fields = grads[1]
        else:
            fields = apply_both(grads[1], left, right)
        nxt = []
        for p in range(count):
            row, block, shift = place(pos, p)
            piece = conj_times(incident(k, p), fields[p])
            add_window(ext, 0, k, row, block, shift, piece[0])
            add_window(ext, 1, k, row, block, shift, piece[1])
            nxt.append(conj_times(pair(win.at[k], p), fields[p]))
        saves.append(fetch(ext.at[:, k], ext_h.at[:, k], sems.at[k]))
        grads = ("inner", nxt)
    return grads[1], saves


def middle_kernel(
    count, pos, wave, win, measured_h, mats_h, exits_h, grad, error, ext_h, ext, psi, measured, mats, exits, sems
):
    slabs = win.shape[0]

    @pl.when(pos[0] == 0)
    def _():
        error[...] = jnp.zeros_like(error)

    @pl.when(pos[0] == 1)
    def _():
        loads = [
            fetch(mats_h, mats, sems.at[slabs]),
            fetch(exits_h, exits, sems.at[slabs + 1]),
            fetch(measured_h, measured, sems.at[slabs + 2]),
        ]
        ext[...] = jnp.zeros_like(ext)
        for copy in loads:
            copy.wait()
        right = (mats[0, 0], mats[0, 1])
        left = (mats[1, 0], mats[1, 1])
        exit_right = (exits[0, 0], exits[0, 1])
        exit_left = (exits[1, 0], exits[1, 1])
        fields = [pair(wave, p) for p in range(count)]
        for k in range(slabs):
            if k:
                for p in range(count):
                    psi[k - 1, p, 0], psi[k - 1, p, 1] = fields[p]
            entering = [times(fields[p], pair(win.at[k], p)) for p in range(count)]
            if k < slabs - 1:
                fields = apply_both(entering, right, left)
            else:
                fields = apply_both(entering, exit_right, exit_left)
        total = jnp.zeros((8, 128), F32)
        far = []
        for p in range(count):
            at = 3 + 2 * count + 2 * p
            target = pltpu.roll(measured[p], (128 - pos[at]) & 127, axis=0)
            target = pltpu.roll(target, (128 - pos[at + 1]) & 127, axis=1)
            re, im = fields[p]
            residual = re * re + im * im - target
            total = total + jnp.sum((residual * residual).reshape(16, 8, 128), axis=0)
            twice = 2.0 * residual
            far.append((twice * re, twice * im))
        error[...] = jnp.full((8, 128), 0.5 * jnp.sum(total), F32)
        entry = apply_both(far, exit_left, exit_right)

        def incident(k, p):
            return pair(wave, p) if k == 0 else pair(psi.at[k - 1], p)

        out, saves = backward_slabs(count, pos, ("exit", entry), win, incident, ext, right, left, ext_h, sems)
        for p in range(count):
            grad[p, 0], grad[p, 1] = out[p]
        for copy in saves:
            copy.wait()


def backward_kernel(
    count, pos, grad, win, psi_h, probe_h, mats_h, ext1_h, error,
    keep, send, ext_h, first, second, ext, probe, mats, psi, sems,
):
    slabs = win.shape[0]

    def packet(re, im):
        upper = jnp.concatenate([im[8:], error[...]], axis=0)
        lower = jnp.concatenate([re, im[:8]], axis=0)

        @pl.when(pos[2] == 0)
        def _():
            keep[...] = lower
            send[0:128, :] = upper
            send[128:136, :] = jnp.zeros((8, 128), F32)

        @pl.when(pos[2] == 1)
        def _():
            keep[0:128, :] = upper
            keep[128:136, :] = jnp.zeros((8, 128), F32)
            send[...] = lower

    @pl.when(pos[0] == 1)
    def _():
        load = fetch(ext1_h, ext, sems.at[0])
        zero = jnp.zeros((WIN, WIN), F32)
        packet(zero, zero)
        load.wait()
        emit_rims(pos, ext, first, second)

    @pl.when(pos[0] == 0)
    def _():
        loads = [
            fetch(mats_h, mats, sems.at[slabs]),
            fetch(psi_h, psi, sems.at[slabs + 1]),
            fetch(probe_h, probe, sems.at[slabs + 2]),
        ]
        ext[...] = jnp.zeros_like(ext)
        for copy in loads:
            copy.wait()
        right = (mats[0, 0], mats[0, 1])
        left = (mats[1, 0], mats[1, 1])

        def incident(k, p):
            return (probe[0], probe[1]) if k == 0 else pair(psi.at[k - 1], p)

        grads = ("inner", [pair(grad, p) for p in range(count)])
        out, saves = backward_slabs(count, pos, grads, win, incident, ext, right, left, ext_h, sems)
        packet(sum(o[0] for o in out[1:]) + out[0][0], sum(o[1] for o in out[1:]) + out[0][1])
        emit_rims(pos, ext, first, second)
        for copy in saves:
            copy.wait()


def fold_rows_kernel(pos, ext_h, row1, row2, first, second, outer, sems):
    loads = [
        fetch(ext_h.at[:, :, pl.ds(64, 128), pl.ds(0, 128)], outer.at[0], sems.at[0]),
        fetch(ext_h.at[:, :, pl.ds(64, 128), pl.ds(384, 128)], outer.at[1], sems.at[1]),
    ]
    for copy in loads:
        copy.wait()
    even = pos[1] == 0
    low = pos[2] * 64
    strip_l = join(roll_half(outer[0, 0]), outer[0, 1])
    strip_r = join(outer[1, 0], roll_half(outer[1, 1]))

    def put(out, strip, lanes):
        out[...] = strip
        for ref, start in ((row1, 64 - low), (row2, low)):
            rows = pl.ds(pl.multiple_of(start, 64), 64)
            out[:, rows, :] = out[:, rows, :] + ref[:, :, lanes]

    @pl.when(even)
    def _():
        put(first, strip_r, slice(640, 768))
        put(second, strip_l, slice(512, 640))

    @pl.when(jnp.logical_not(even))
    def _():
        put(first, strip_l, slice(512, 640))
        put(second, strip_r, slice(640, 768))


def fold_kernel(pos, ext_h, row1, row2, col1, col2, out, sems):
    fetch(ext_h.at[:, :, pl.ds(64, 128), pl.ds(128, 256)], out, sems.at[0]).wait()
    even = pos[1] == 0
    low = pos[2] * 64
    for ref, start in ((row1, 64 - low), (row2, low)):
        rows = pl.ds(pl.multiple_of(start, 64), 64)
        out[0, :, rows, :] = out[0, :, rows, :] + ref[:, :, 0:256]
        out[1, :, rows, :] = out[1, :, rows, :] + ref[:, :, 256:512]

    def columns(from_left, from_right):
        zero = jnp.zeros(from_left.shape, F32)
        out[0, :, :, :128] = out[0, :, :, :128] + join(from_left[...], zero)
        out[1, :, :, :128] = out[1, :, :, :128] + join(roll_half(from_left[...]), zero)
        out[0, :, :, 128:] = out[0, :, :, 128:] + join(zero, roll_half(from_right[...]))
        out[1, :, :, 128:] = out[1, :, :, 128:] + join(zero, from_right[...])

    @pl.when(even)
    def _():
        columns(col2, col1)

    @pl.when(jnp.logical_not(even))
    def _():
        columns(col1, col2)


def finish_kernel(scales, pos, keep, back, probe, error):
    def put(lower, upper):
        probe[0] = lower[0:128, :] * scales[0]
        probe[1, 0:8, :] = lower[128:136, :] * scales[0]
        probe[1, 8:128, :] = upper[0:120, :] * scales[0]
        error[0, 0] = jnp.max(upper[120:128, :]) * scales[1]

    @pl.when(pos[2] == 0)
    def _():
        put(keep, back)

    @pl.when(pos[2] == 1)
    def _():
        put(back, keep)


HBM = pltpu.MemorySpace.HBM
VMEM = pltpu.MemorySpace.VMEM


def call(kernel, outs, scalars, arrays, scratch=(), flops=0, hbm=(), hbm_out=(), smem_out=(), fixed=(), aliases=None):
    outs = [jax.ShapeDtypeStruct(s, F32) for s in outs]
    moved = sum(int(np.prod(a.shape)) * 4 for a in list(arrays) + outs)
    arrays = [pltpu.with_memory_space_constraint(a, HBM) if i in fixed else a for i, a in enumerate(arrays)]
    return pl.pallas_call(
        kernel,
        out_shape=outs,
        in_specs=[pl.BlockSpec(memory_space=pltpu.SMEM)] * len(scalars)
        + [pl.BlockSpec(memory_space=HBM if i in hbm else VMEM) for i in range(len(arrays))],
        out_specs=[
            pl.BlockSpec(memory_space=HBM if i in hbm_out else pltpu.SMEM if i in smem_out else VMEM)
            for i in range(len(outs))
        ],
        scratch_shapes=list(scratch),
        input_output_aliases=aliases or {},
        compiler_params=pltpu.CompilerParams(vmem_limit_bytes=VMEM_LIMIT),
        cost_estimate=pl.CostEstimate(flops=flops, bytes_accessed=moved, transcendentals=0),
    )(*scalars, *arrays)


def swap(value, axis, odd=False):
    size = lax.axis_size(axis)
    pairs = [(i, ((i - 1) ^ 1) + 1) for i in range(1, size - 1)] if odd else [(i, i ^ 1) for i in range(size)]
    return lax.ppermute(value, axis, pairs)


AXES = ("sx", "sy", "depth")


def ring_sum(value, sizes, turn):
    rows, cols, depth = sizes

    def flat(a, b, d):
        return (a * cols + b) * depth + d

    got = []
    for step in (1, 2, 3):
        pairs = [
            (flat(a, b, d), flat(*turn(a, b, d, step))) for a in range(rows) for b in range(cols) for d in range(depth)
        ]
        got.append(lax.ppermute(value, AXES, pairs))
    return (value + got[1]) + (got[0] + got[2])


def turn_x(a, b, d, step):
    return a, b // 4 * 4 + (b + step) % 4, d


def turn_z(a, b, d, step):
    return a, (b // 4 + step) % 4 * 4 + b % 4, d


def turn_y(a, b, d, step):
    y = (a // 2 * 2 + d + step) % 4
    return y // 2 * 2 + a % 2, b, y % 2


def local(probe_wave, transmission, scan_offsets, pattern_shifts, patterns):
    slabs, rows, cols = transmission.shape[1:]
    count = scan_offsets.shape[2]
    measured = patterns.reshape(count, WIN, WIN)
    steps, exits = constants()
    core = lax.axis_index("sx") % 2
    where = jnp.stack([lax.axis_index("depth"), lax.axis_index("sy") % 2, core]).astype(jnp.int32)
    pos = jnp.concatenate([where, scan_offsets.reshape(-1), pattern_shifts.reshape(-1)])
    sizes = (lax.axis_size("sx"), lax.axis_size("sy"), lax.axis_size("depth"))

    tile = (2, slabs, rows, cols)
    strip = (slabs, rows, 128)
    rim = (slabs, HALF, 768)
    side = (2, slabs, HALF, cols)
    corner = (slabs, HALF, 256)
    field = (count, 2, WIN, WIN)
    inner = (slabs - 1,) + field
    ext = (2, slabs, rows + 2 * HALF + 8, 512)
    step_flops = 2 * 3 * 2 * 256 * 256 * WIN * count

    def vmem(shape, dtype=F32):
        return pltpu.VMEM(shape, dtype)

    def sems(n):
        return pltpu.SemaphoreType.DMA((n,))

    mats = vmem(steps.shape, BF16)
    probe = vmem(probe_wave.shape)

    col1, col2, row1, row2 = call(
        pack_kernel, [strip, strip, side, side], [where], [transmission], [vmem(tile), sems(1)], hbm=(0,), fixed=(0,)
    )
    col1, col2 = swap(col1, "sy"), swap(col2, "sy", True)
    row1, row2 = swap(row1, "sx"), swap(row2, "sx", True)
    crn1, crn2 = call(pack_corners_kernel, [corner, corner], [where], [col1, col2])
    crn1, crn2 = swap(crn1, "sx"), swap(crn2, "sx", True)
    wave, win, psi = call(
        functools.partial(forward_kernel, count),
        [field, (slabs,) + field, inner],
        [pos],
        [probe_wave, transmission, col1, col2, row1, row2, crn1, crn2, steps],
        [vmem(ext), probe, mats, vmem(inner), vmem((2,) + strip), vmem((2,) + corner), sems(slabs + 8)],
        slabs * step_flops,
        hbm=tuple(range(9)),
        fixed=(0, 1, 8),
        hbm_out=(2,),
    )
    wave = lax.ppermute(wave, "depth", [(0, 1)])
    grad, error, edge = call(
        functools.partial(middle_kernel, count),
        [field, (8, 128), ext],
        [pos],
        [wave, win, measured, steps, exits],
        [vmem(ext), vmem(inner), vmem(measured.shape), mats, mats, sems(slabs + 3)],
        2 * slabs * step_flops,
        hbm=(2, 3, 4),
        fixed=(2, 3, 4),
        hbm_out=(2,),
    )
    grad = lax.ppermute(grad, "depth", [(1, 0)])
    part, other, edge, row1, row2 = call(
        functools.partial(backward_kernel, count),
        [(136, WIN), (136, WIN), ext, rim, rim],
        [pos],
        [grad, win, psi, probe_wave, steps, edge, error],
        [vmem(ext), probe, mats, vmem(inner), sems(slabs + 3)],
        slabs * step_flops,
        hbm=(2, 3, 4, 5),
        fixed=(3, 4),
        hbm_out=(2,),
        aliases={6: 2},
    )
    row1, row2 = swap(row1, "sx"), swap(row2, "sx", True)
    part = part + swap(other, "sx")
    part = ring_sum(part, sizes, turn_x)
    part, row1, row2 = lax.optimization_barrier((part, row1, row2))
    col1, col2 = call(
        fold_rows_kernel, [strip, strip], [where], [edge, row1, row2],
        [vmem((2, 2) + strip), sems(2)], hbm=(0,),
    )
    part, col1, col2 = lax.optimization_barrier((part, col1, col2))
    col1, col2 = swap(col1, "sy"), swap(col2, "sy", True)
    part = ring_sum(part, sizes, turn_z)
    part, col1, col2 = lax.optimization_barrier((part, col1, col2))
    (out,) = call(fold_kernel, [tile], [where], [edge, row1, row2, col1, col2], [sems(1)], hbm=(0,))
    part = ring_sum(part, sizes, turn_y)
    other = swap(part, "sx")
    positions = count * sizes[0] * sizes[1]
    scales = jnp.array([1.0 / positions, 1.0 / (positions * WIN * WIN)], F32)
    probe_grad, error = call(finish_kernel, [(2, WIN, WIN), (1, 1)], [scales, where], [part, other], smem_out=(1,))
    return out, probe_grad, error.reshape(())


def solution(mesh):
    in_specs = (
        P(),
        P(None, "depth", "sx", "sy"),
        P("sx", "sy", None, None),
        P("sx", "sy", None, None),
        P("sx", "sy", None, None, None),
    )
    out_specs = (P(None, "depth", "sx", "sy"), P(), P())
    return jax.shard_map(local, mesh=mesh, in_specs=in_specs, out_specs=out_specs, check_vma=False)
```

profile of v0, /device:TPU:33, one launch (start us, length us, event | category | flops | bytes accessed | tf_op | source)
XLA Modules:
  0.0 118.5 jit_solution(7130258343159599335)
XLA Ops:
  0.7 2.1 %shard_map.103 = (f32[4,128,128]{2,1,0:T(8,128)S(1)}, f32[4,128,128]{2,1,0:T(8,128)S(1)}, f32[2,4,64,256]{3,2,1,0:T(8,128)S(1)}, f32[2,4,64,256]{3,2,1,0:T(8,128)S(1)}) custom-call(s32[3]{0:T(128)S(1)} %pad_add_fusion.pos, f32[2,4,128,256]{3,2,1,0:T(8,128)} %tile.1), custom_call_target="tpu_custom_call" | custom-call | bytes 2621440 | tf_op jit(solution)/shard_map/pallas_call | solution.py:456
  4.1 3.3 %collective-permute-start.1 = (f32[4,128,128]{2,1,0:T(8,128)S(1)}, f32[4,128,128]{2,1,0:T(8,128)S(1)}, u32[]{:S(2)}, u32[]{:S(2)}) collective-permute-start(f32[4,128,128]{2,1,0:T(8,128)S(1)} %get-tuple-element.34), channel_id=1, source_target_pairs={{2,4},{4,2},{6,8},{8,6},{10,12},{12,10},{14,16},{16,14},{18,20},{2... | collective-permute-start | bytes 786440 | tf_op jit(solution)/shard_map/ppermute | solution.py:475
  8.7 4.7 %collective-permute-start.3 = (f32[2,4,64,256]{3,2,1,0:T(8,128)S(1)}, f32[2,4,64,256]{3,2,1,0:T(8,128)S(1)}, u32[]{:S(2)}, u32[]{:S(2)}) collective-permute-start(f32[2,4,64,256]{3,2,1,0:T(8,128)S(1)} %get-tuple-element.36), channel_id=1, source_target_pairs={{32,64},{64,32},{33,65},{65,33},{34,66},{66,34},{35,67},{67,35},{3... | collective-permute-start | bytes 1572872 | tf_op jit(solution)/shard_map/ppermute | solution.py:475
  13.4 1.6 %collective-permute-done.1.col2.col2_h = f32[4,128,128]{2,1,0:T(8,128)S(1)} collective-permute-done((f32[4,128,128]{2,1,0:T(8,128)S(1)}, f32[4,128,128]{2,1,0:T(8,128)S(1)}, u32[]{:S(2)}, u32[]{:S(2)}) %collective-permute-start.1) | collective-permute-done | bytes 262176 | tf_op jit(solution)/shard_map/ppermute | solution.py:475
  16.3 1.8 %collective-permute-start.4 = (f32[4,64,256]{2,1,0:T(8,128)}, f32[4,64,256]{2,1,0:T(8,128)S(1)}, u32[]{:S(2)}, u32[]{:S(2)}) collective-permute-start(f32[4,64,256]{2,1,0:T(8,128)} %get-tuple-element.37), channel_id=1, source_target_pairs={{0,32},{32,0},{64,96},{96,64},{1,33},{33,1},{65,97},{97,65},{2,34}... | collective-permute-start | bytes 786440 | tf_op jit(solution)/shard_map/ppermute | solution.py:475
  18.1 4.7 %collective-permute-start.5 = (f32[4,64,256]{2,1,0:T(8,128)S(1)}, f32[4,64,256]{2,1,0:T(8,128)S(1)}, u32[]{:S(2)}, u32[]{:S(2)}) collective-permute-start(f32[4,64,256]{2,1,0:T(8,128)S(1)} %get-tuple-element.38), channel_id=1, source_target_pairs={{32,64},{64,32},{33,65},{65,33},{34,66},{66,34},{35,67},{67,35},{3... | collective-permute-start | bytes 786440 | tf_op jit(solution)/shard_map/ppermute | solution.py:475
  24.6 2.7 %collective-permute-done.5.crn2_h = f32[4,64,256]{2,1,0:T(8,128)S(1)} collective-permute-done((f32[4,64,256]{2,1,0:T(8,128)S(1)}, f32[4,64,256]{2,1,0:T(8,128)S(1)}, u32[]{:S(2)}, u32[]{:S(2)}) %collective-permute-start.5) | collective-permute-done | bytes 262176 | tf_op jit(solution)/shard_map/ppermute | solution.py:475
  27.3 7.6 %shard_map.105 = (f32[4,2,128,128]{3,2,1,0:T(8,128)S(1)}, f32[4,4,2,128,128]{4,3,2,1,0:T(8,128)S(1)}, f32[3,4,2,128,128]{4,3,2,1,0:T(8,128)S(1)}) custom-call(s32[19]{0:T(128)S(1)} %concatenate.4.pos, f32[2,128,128]{2,1,0:T(8,128)} %probe_h.3, f32[2,4,128,256]{3,2,1,0:T(8,128)} %tile.1, f32[4,128,128]{2,1,0:T(8,128)S(1)} %collective-permute-done.col1.col1_h, ...), custom_call_target="tpu_custom_call" | custom-call | flops 1610612736 | bytes 8519680 | tf_op jit(solution)/shard_map/pallas_call | solution.py:456
  36.2 6.1 %collective-permute-done.6.wave = f32[4,2,128,128]{3,2,1,0:T(8,128)S(1)} collective-permute-done((f32[4,2,128,128]{3,2,1,0:T(8,128)S(1)}, f32[4,2,128,128]{3,2,1,0:T(8,128)S(1)}, u32[]{:S(2)}, u32[]{:S(2)}) %collective-permute-start.6) | collective-permute-done | bytes 524320 | tf_op jit(solution)/shard_map/ppermute | solution.py:556
  44.4 19.2 %collective-permute-done.7.grad = f32[4,2,128,128]{3,2,1,0:T(8,128)S(1)} collective-permute-done((f32[4,2,128,128]{3,2,1,0:T(8,128)S(1)}, f32[4,2,128,128]{3,2,1,0:T(8,128)S(1)}, u32[]{:S(2)}, u32[]{:S(2)}) %collective-permute-start.7) | collective-permute-done | bytes 524320 | tf_op jit(solution)/shard_map/ppermute | solution.py:568
  63.6 7.9 %shard_map.107 = (f32[136,128]{1,0:T(8,128)S(1)}, f32[136,128]{1,0:T(8,128)S(1)}, f32[2,4,264,512]{3,2,1,0:T(8,128)S(1)}, f32[4,64,768]{2,1,0:T(8,128)S(1)}, f32[4,64,768]{2,1,0:T(8,128)S(1)}) custom-call(s32[19]{0:T(128)S(1)} %concatenate.4.pos, f32[4,2,128,128]{3,2,1,0:T(8,128)S(1)} %collective-permute-done.7.grad, ...), custom_call_target="tpu_custom_call", output_to_operand_aliasing={{2}: (6, {})} | custom-call | flops 1610612736 | bytes 15740928 | tf_op jit(solution)/shard_map/pallas_call | solution.py:456
  71.7 6.5 %collective-permute-start.13 = (f32[4,64,768]{2,1,0:T(8,128)S(1)}, f32[4,64,768]{2,1,0:T(8,128)S(1)}, u32[]{:S(2)}, u32[]{:S(2)}) collective-permute-start(f32[4,64,768]{2,1,0:T(8,128)S(1)} %get-tuple-element.49), channel_id=1, source_target_pairs={{32,64},{64,32},{33,65},{65,33},{34,66},{66,34},{35,67},{67,35},{3... | collective-permute-start | bytes 2359304 | tf_op jit(solution)/shard_map/ppermute | solution.py:475
  79.5 1.9 %collective-permute-start.11 = (f32[136,128]{1,0:T(8,128)S(1)}, f32[136,128]{1,0:T(8,128)S(1)}, u32[]{:S(2)}, u32[]{:S(2)}) collective-permute-start(f32[136,128]{1,0:T(8,128)S(1)} %add.39), channel_id=1, source_target_pairs={{0,6},{1,7},{2,0},{3,1},{4,2},{5,3},{6,4},{7,5},{8,14},{9,15},{10,... | collective-permute-start | bytes 208904 | tf_op jit(solution)/shard_map/ppermute | solution.py:492
  83.2 4.7 %collective-permute-done.10 = f32[136,128]{1,0:T(8,128)S(1)} collective-permute-done((f32[136,128]{1,0:T(8,128)S(1)}, f32[136,128]{1,0:T(8,128)S(1)}, u32[]{:S(2)}, u32[]{:S(2)}) %collective-permute-start.10) | collective-permute-done | bytes 69664 | tf_op jit(solution)/shard_map/ppermute | solution.py:492
  89.0 1.7 %collective-permute-start.15 = (f32[136,128]{1,0:T(8,128)S(1)}, f32[136,128]{1,0:T(8,128)S(1)}, u32[]{:S(2)}, u32[]{:S(2)}) collective-permute-start(f32[136,128]{1,0:T(8,128)S(1)} %add_add_fusion.2), channel_id=1, source_target_pairs={{0,8},{1,9},{2,10},{3,11},{4,12},{5,13},{6,14},{7,15},{8,16},{9,17... | collective-permute-start | bytes 208904 | tf_op jit(solution)/shard_map/ppermute | solution.py:492
  90.7 3.5 %collective-permute-start.14 = (f32[136,128]{1,0:T(8,128)S(1)}, f32[136,128]{1,0:T(8,128)S(1)}, u32[]{:S(2)}, u32[]{:S(2)}) collective-permute-start(f32[136,128]{1,0:T(8,128)S(1)} %add_add_fusion.2), channel_id=1, source_target_pairs={{0,16},{1,17},{2,18},{3,19},{4,20},{5,21},{6,22},{7,23},{8,24},{9,... | collective-permute-start | bytes 208904 | tf_op jit(solution)/shard_map/ppermute | solution.py:492
  94.2 3.3 %collective-permute-start.18 = (f32[4,128,128]{2,1,0:T(8,128)S(1)}, f32[4,128,128]{2,1,0:T(8,128)S(1)}, u32[]{:S(2)}, u32[]{:S(2)}) collective-permute-start(f32[4,128,128]{2,1,0:T(8,128)S(1)} %get-tuple-element.57), channel_id=1, source_target_pairs={{2,4},{4,2},{6,8},{8,6},{10,12},{12,10},{14,16},{16,14},{18,20},{2... | collective-permute-start | bytes 786440 | tf_op jit(solution)/shard_map/ppermute | solution.py:475
  97.6 3.9 %collective-permute-done.17.col1 = f32[4,128,128]{2,1,0:T(8,128)S(1)} collective-permute-done((f32[4,128,128]{2,1,0:T(8,128)S(1)}, f32[4,128,128]{2,1,0:T(8,128)S(1)}, u32[]{:S(2)}, u32[]{:S(2)}) %collective-permute-start.17) | collective-permute-done | bytes 262176 | tf_op jit(solution)/shard_map/ppermute | solution.py:475
  101.5 4.0 %collective-permute-done.18.col2 = f32[4,128,128]{2,1,0:T(8,128)S(1)} collective-permute-done((f32[4,128,128]{2,1,0:T(8,128)S(1)}, f32[4,128,128]{2,1,0:T(8,128)S(1)}, u32[]{:S(2)}, u32[]{:S(2)}) %collective-permute-start.18) | collective-permute-done | bytes 262176 | tf_op jit(solution)/shard_map/ppermute | solution.py:475
  105.4 1.5 %collective-permute-start.20 = (f32[136,128]{1,0:T(8,128)S(1)}, f32[136,128]{1,0:T(8,128)S(1)}, u32[]{:S(2)}, u32[]{:S(2)}) collective-permute-start(f32[136,128]{1,0:T(8,128)S(1)} %add_add_fusion.1), channel_id=1, source_target_pairs={{0,1},{1,64},{2,3},{3,66},{4,5},{5,68},{6,7},{7,70},{8,9},{9,72},{... | collective-permute-start | bytes 208904 | tf_op jit(solution)/shard_map/ppermute | solution.py:492
  106.9 1.7 %collective-permute-done.21 = f32[136,128]{1,0:T(8,128)S(1)} collective-permute-done((f32[136,128]{1,0:T(8,128)S(1)}, f32[136,128]{1,0:T(8,128)S(1)}, u32[]{:S(2)}, u32[]{:S(2)}) %collective-permute-start.21) | collective-permute-done | bytes 69664 | tf_op jit(solution)/shard_map/ppermute | solution.py:492
  109.8 1.8 %collective-permute-done.19 = f32[136,128]{1,0:T(8,128)S(1)} collective-permute-done((f32[136,128]{1,0:T(8,128)S(1)}, f32[136,128]{1,0:T(8,128)S(1)}, u32[]{:S(2)}, u32[]{:S(2)}) %collective-permute-start.19) | collective-permute-done | bytes 69664 | tf_op jit(solution)/shard_map/ppermute | solution.py:492
  111.6 3.2 %collective-permute-start.22 = (f32[136,128]{1,0:T(8,128)S(1)}, f32[136,128]{1,0:T(8,128)S(1)}, u32[]{:S(2)}, u32[]{:S(2)}) collective-permute-start(f32[136,128]{1,0:T(8,128)S(1)} %add_add_fusion.keep), channel_id=1, source_target_pairs={{0,32},{32,0},{64,96},{96,64},{1,33},{33,1},{65,97},{97,65},{2,34}... | collective-permute-start | bytes 208904 | tf_op jit(solution)/shard_map/ppermute | solution.py:475
  114.9 2.0 %shard_map.109 = f32[2,4,128,256]{3,2,1,0:T(8,128)} custom-call(s32[3]{0:T(128)S(1)} %pad_add_fusion.pos, f32[2,4,264,512]{3,2,1,0:T(8,128)S(1)} %get-tuple-element.45.ext_h, f32[4,64,768]{2,1,0:T(8,128)S(1)} %collective-permute-done.12.row1, f32[4,64,768]{2,1,0:T(8,128)S(1)} %collective-permute-done.13.row2, ...), custom_call_target="tpu_custom_call" | custom-call | bytes 7471104 | tf_op jit(solution)/shard_map/pallas_call | solution.py:456
  (42 shorter events, 16.1 us)
Async XLA Ops:
  2.8 10.6 %collective-permute-start = (f32[4,128,128]{2,1,0:T(8,128)S(1)}, f32[4,128,128]{2,1,0:T(8,128)S(1)}, u32[]{:S(2)}, u32[]{:S(2)}) collective-permute-start(f32[4,128,128]{2,1,0:T(8,128)S(1)} %get-tuple-element.33), channel_id=1, source_target_pairs={{0,2},{2,0},{4,6},{6,4},{8,10},{10,8},{12,14},{14,12},{16,18},{18,... | collective-permute-start | bytes 786440 | tf_op jit(solution)/shard_map/ppermute | solution.py:475
  4.1 10.9 %collective-permute-start.1 = (f32[4,128,128]{2,1,0:T(8,128)S(1)}, f32[4,128,128]{2,1,0:T(8,128)S(1)}, u32[]{:S(2)}, u32[]{:S(2)}) collective-permute-start(f32[4,128,128]{2,1,0:T(8,128)S(1)} %get-tuple-element.34), channel_id=1, source_target_pairs={{2,4},{4,2},{6,8},{8,6},{10,12},{12,10},{14,16},{16,14},{18,20},{2... | collective-permute-start | bytes 786440 | tf_op jit(solution)/shard_map/ppermute | solution.py:475
  7.4 19.9 %collective-permute-start.2 = (f32[2,4,64,256]{3,2,1,0:T(8,128)S(1)}, f32[2,4,64,256]{3,2,1,0:T(8,128)S(1)}, u32[]{:S(2)}, u32[]{:S(2)}) collective-permute-start(f32[2,4,64,256]{3,2,1,0:T(8,128)S(1)} %get-tuple-element.35), channel_id=1, source_target_pairs={{0,32},{32,0},{64,96},{96,64},{1,33},{33,1},{65,97},{97,65},{2,34}... | collective-permute-start | bytes 1572872 | tf_op jit(solution)/shard_map/ppermute | solution.py:475
  8.7 18.6 %collective-permute-start.3 = (f32[2,4,64,256]{3,2,1,0:T(8,128)S(1)}, f32[2,4,64,256]{3,2,1,0:T(8,128)S(1)}, u32[]{:S(2)}, u32[]{:S(2)}) collective-permute-start(f32[2,4,64,256]{3,2,1,0:T(8,128)S(1)} %get-tuple-element.36), channel_id=1, source_target_pairs={{32,64},{64,32},{33,65},{65,33},{34,66},{66,34},{35,67},{67,35},{3... | collective-permute-start | bytes 1572872 | tf_op jit(solution)/shard_map/ppermute | solution.py:475
  16.3 8.3 %collective-permute-start.4 = (f32[4,64,256]{2,1,0:T(8,128)}, f32[4,64,256]{2,1,0:T(8,128)S(1)}, u32[]{:S(2)}, u32[]{:S(2)}) collective-permute-start(f32[4,64,256]{2,1,0:T(8,128)} %get-tuple-element.37), channel_id=1, source_target_pairs={{0,32},{32,0},{64,96},{96,64},{1,33},{33,1},{65,97},{97,65},{2,34}... | collective-permute-start | bytes 786440 | tf_op jit(solution)/shard_map/ppermute | solution.py:475
  18.1 9.2 %collective-permute-start.5 = (f32[4,64,256]{2,1,0:T(8,128)S(1)}, f32[4,64,256]{2,1,0:T(8,128)S(1)}, u32[]{:S(2)}, u32[]{:S(2)}) collective-permute-start(f32[4,64,256]{2,1,0:T(8,128)S(1)} %get-tuple-element.38), channel_id=1, source_target_pairs={{32,64},{64,32},{33,65},{65,33},{34,66},{66,34},{35,67},{67,35},{3... | collective-permute-start | bytes 786440 | tf_op jit(solution)/shard_map/ppermute | solution.py:475
  34.9 7.4 %collective-permute-start.6 = (f32[4,2,128,128]{3,2,1,0:T(8,128)S(1)}, f32[4,2,128,128]{3,2,1,0:T(8,128)S(1)}, u32[]{:S(2)}, u32[]{:S(2)}) collective-permute-start(f32[4,2,128,128]{3,2,1,0:T(8,128)S(1)} %get-tuple-element.39), channel_id=1, source_target_pairs={{0,1},{2,3},{4,5},{6,7},{8,9},{10,11},{12,13},{14,15},{16,17},{18,... | collective-permute-start | bytes 1572872 | tf_op jit(solution)/shard_map/ppermute | solution.py:556
  43.1 20.5 %collective-permute-start.7 = (f32[4,2,128,128]{3,2,1,0:T(8,128)S(1)}, f32[4,2,128,128]{3,2,1,0:T(8,128)S(1)}, u32[]{:S(2)}, u32[]{:S(2)}) collective-permute-start(f32[4,2,128,128]{3,2,1,0:T(8,128)S(1)} %get-tuple-element.41), channel_id=1, source_target_pairs={{1,0},{3,2},{5,4},{7,6},{9,8},{11,10},{13,12},{15,14},{17,16},{19,... | collective-permute-start | bytes 1572872 | tf_op jit(solution)/shard_map/ppermute | solution.py:568
  71.6 16.3 %collective-permute-start.12 = (f32[4,64,768]{2,1,0:T(8,128)S(1)}, f32[4,64,768]{2,1,0:T(8,128)S(1)}, u32[]{:S(2)}, u32[]{:S(2)}) collective-permute-start(f32[4,64,768]{2,1,0:T(8,128)S(1)} %get-tuple-element.48), channel_id=1, source_target_pairs={{0,32},{32,0},{64,96},{96,64},{1,33},{33,1},{65,97},{97,65},{2,34}... | collective-permute-start | bytes 2359304 | tf_op jit(solution)/shard_map/ppermute | solution.py:475
  71.7 16.2 %collective-permute-start.13 = (f32[4,64,768]{2,1,0:T(8,128)S(1)}, f32[4,64,768]{2,1,0:T(8,128)S(1)}, u32[]{:S(2)}, u32[]{:S(2)}) collective-permute-start(f32[4,64,768]{2,1,0:T(8,128)S(1)} %get-tuple-element.49), channel_id=1, source_target_pairs={{32,64},{64,32},{33,65},{65,33},{34,66},{66,34},{35,67},{67,35},{3... | collective-permute-start | bytes 2359304 | tf_op jit(solution)/shard_map/ppermute | solution.py:475
  78.1 1.3 %collective-permute-start.8 = (f32[136,128]{1,0:T(8,128)S(1)}, f32[136,128]{1,0:T(8,128)S(1)}, u32[]{:S(2)}, u32[]{:S(2)}) collective-permute-start(f32[136,128]{1,0:T(8,128)S(1)} %get-tuple-element.47), channel_id=1, source_target_pairs={{0,32},{32,0},{64,96},{96,64},{1,33},{33,1},{65,97},{97,65},{2,34}... | collective-permute-start | bytes 208904 | tf_op jit(solution)/shard_map/ppermute | solution.py:475
  79.5 3.6 %collective-permute-start.11 = (f32[136,128]{1,0:T(8,128)S(1)}, f32[136,128]{1,0:T(8,128)S(1)}, u32[]{:S(2)}, u32[]{:S(2)}) collective-permute-start(f32[136,128]{1,0:T(8,128)S(1)} %add.39), channel_id=1, source_target_pairs={{0,6},{1,7},{2,0},{3,1},{4,2},{5,3},{6,4},{7,5},{8,14},{9,15},{10,... | collective-permute-start | bytes 208904 | tf_op jit(solution)/shard_map/ppermute | solution.py:492
  81.4 6.5 %collective-permute-start.10 = (f32[136,128]{1,0:T(8,128)S(1)}, f32[136,128]{1,0:T(8,128)S(1)}, u32[]{:S(2)}, u32[]{:S(2)}) collective-permute-start(f32[136,128]{1,0:T(8,128)S(1)} %add.39), channel_id=1, source_target_pairs={{0,2},{1,3},{2,4},{3,5},{4,6},{5,7},{6,0},{7,1},{8,10},{9,11},{10,... | collective-permute-start | bytes 208904 | tf_op jit(solution)/shard_map/ppermute | solution.py:492
  81.4 6.5 %collective-permute-start.9 = (f32[136,128]{1,0:T(8,128)S(1)}, f32[136,128]{1,0:T(8,128)S(1)}, u32[]{:S(2)}, u32[]{:S(2)}) collective-permute-start(f32[136,128]{1,0:T(8,128)S(1)} %add.39), channel_id=1, source_target_pairs={{0,4},{1,5},{2,6},{3,7},{4,0},{5,1},{6,2},{7,3},{8,12},{9,13},{10,... | collective-permute-start | bytes 208904 | tf_op jit(solution)/shard_map/ppermute | solution.py:492
  88.9 28.0 %copy-start = (f32[2]{0:T(128)S(1)}, f32[2]{0:T(128)}, u32[]{:S(2)}) copy-start(f32[2]{0:T(128)} %constant.39.clone.scales) | copy-start | bytes 28
  88.9 8.6 %collective-permute-start.16 = (f32[136,128]{1,0:T(8,128)S(1)}, f32[136,128]{1,0:T(8,128)S(1)}, u32[]{:S(2)}, u32[]{:S(2)}) collective-permute-start(f32[136,128]{1,0:T(8,128)S(1)} %add_add_fusion.2), channel_id=1, source_target_pairs={{0,24},{1,25},{2,26},{3,27},{4,28},{5,29},{6,30},{7,31},{8,0},{9,1... | collective-permute-start | bytes 208904 | tf_op jit(solution)/shard_map/ppermute | solution.py:492
  89.0 8.5 %collective-permute-start.15 = (f32[136,128]{1,0:T(8,128)S(1)}, f32[136,128]{1,0:T(8,128)S(1)}, u32[]{:S(2)}, u32[]{:S(2)}) collective-permute-start(f32[136,128]{1,0:T(8,128)S(1)} %add_add_fusion.2), channel_id=1, source_target_pairs={{0,8},{1,9},{2,10},{3,11},{4,12},{5,13},{6,14},{7,15},{8,16},{9,17... | collective-permute-start | bytes 208904 | tf_op jit(solution)/shard_map/ppermute | solution.py:492
  90.7 6.8 %collective-permute-start.14 = (f32[136,128]{1,0:T(8,128)S(1)}, f32[136,128]{1,0:T(8,128)S(1)}, u32[]{:S(2)}, u32[]{:S(2)}) collective-permute-start(f32[136,128]{1,0:T(8,128)S(1)} %add_add_fusion.2), channel_id=1, source_target_pairs={{0,16},{1,17},{2,18},{3,19},{4,20},{5,21},{6,22},{7,23},{8,24},{9,... | collective-permute-start | bytes 208904 | tf_op jit(solution)/shard_map/ppermute | solution.py:492
  94.2 7.2 %collective-permute-start.17 = (f32[4,128,128]{2,1,0:T(8,128)S(1)}, f32[4,128,128]{2,1,0:T(8,128)S(1)}, u32[]{:S(2)}, u32[]{:S(2)}) collective-permute-start(f32[4,128,128]{2,1,0:T(8,128)S(1)} %get-tuple-element.56), channel_id=1, source_target_pairs={{0,2},{2,0},{4,6},{6,4},{8,10},{10,8},{12,14},{14,12},{16,18},{18,... | collective-permute-start | bytes 786440 | tf_op jit(solution)/shard_map/ppermute | solution.py:475
  94.2 11.2 %collective-permute-start.18 = (f32[4,128,128]{2,1,0:T(8,128)S(1)}, f32[4,128,128]{2,1,0:T(8,128)S(1)}, u32[]{:S(2)}, u32[]{:S(2)}) collective-permute-start(f32[4,128,128]{2,1,0:T(8,128)S(1)} %get-tuple-element.57), channel_id=1, source_target_pairs={{2,4},{4,2},{6,8},{8,6},{10,12},{12,10},{14,16},{16,14},{18,20},{2... | collective-permute-start | bytes 786440 | tf_op jit(solution)/shard_map/ppermute | solution.py:475
  105.4 3.2 %collective-permute-start.21 = (f32[136,128]{1,0:T(8,128)S(1)}, f32[136,128]{1,0:T(8,128)S(1)}, u32[]{:S(2)}, u32[]{:S(2)}) collective-permute-start(f32[136,128]{1,0:T(8,128)S(1)} %add_add_fusion.1), channel_id=1, source_target_pairs={{0,65},{1,0},{2,67},{3,2},{4,69},{5,4},{6,71},{7,6},{8,73},{9,8},{... | collective-permute-start | bytes 208904 | tf_op jit(solution)/shard_map/ppermute | solution.py:492
  105.4 4.4 %collective-permute-start.20 = (f32[136,128]{1,0:T(8,128)S(1)}, f32[136,128]{1,0:T(8,128)S(1)}, u32[]{:S(2)}, u32[]{:S(2)}) collective-permute-start(f32[136,128]{1,0:T(8,128)S(1)} %add_add_fusion.1), channel_id=1, source_target_pairs={{0,1},{1,64},{2,3},{3,66},{4,5},{5,68},{6,7},{7,70},{8,9},{9,72},{... | collective-permute-start | bytes 208904 | tf_op jit(solution)/shard_map/ppermute | solution.py:492
  106.9 4.7 %collective-permute-start.19 = (f32[136,128]{1,0:T(8,128)S(1)}, f32[136,128]{1,0:T(8,128)S(1)}, u32[]{:S(2)}, u32[]{:S(2)}) collective-permute-start(f32[136,128]{1,0:T(8,128)S(1)} %add_add_fusion.1), channel_id=1, source_target_pairs={{0,64},{1,65},{2,66},{3,67},{4,68},{5,69},{6,70},{7,71},{8,72},{9,... | collective-permute-start | bytes 208904 | tf_op jit(solution)/shard_map/ppermute | solution.py:492
  111.6 5.3 %collective-permute-start.22 = (f32[136,128]{1,0:T(8,128)S(1)}, f32[136,128]{1,0:T(8,128)S(1)}, u32[]{:S(2)}, u32[]{:S(2)}) collective-permute-start(f32[136,128]{1,0:T(8,128)S(1)} %add_add_fusion.keep), channel_id=1, source_target_pairs={{0,32},{32,0},{64,96},{96,64},{1,33},{33,1},{65,97},{97,65},{2,34}... | collective-permute-start | bytes 208904 | tf_op jit(solution)/shard_map/ppermute | solution.py:475
where the time goes:
time: 119 us; the launch traced here: 118 us
  waiting for transfers between devices  48.7 us (41%)
  starting transfers between devices  42.8 us (36%)
  Pallas kernels  24.1 us (20%)
  local copies, waits for them, and re-layouts  1.79 us (2%)
    ppermute x12, starting transfers between devices, swap(): return lax.ppermute(value, axis, pairs)  30.2 us
    pallas_call x8, Pallas kernels, call(): pl.pallas_call(kernel, out_shape=outs, in_specs=[pl.BlockSpec(memory_spac...  24.1 us
    ppermute x1, waiting for transfers between devices, local(): grad = lax.ppermute(grad, 'depth', [(1, 0)])  19.2 us
    ppermute x12, waiting for transfers between devices, swap(): return lax.ppermute(value, axis, pairs)  13.4 us
    ppermute x9, waiting for transfers between devices, ring_sum(): got.append(lax.ppermute(value, AXES, pairs))  9.96 us
    ppermute x9, starting transfers between devices, ring_sum(): got.append(lax.ppermute(value, AXES, pairs))  9.91 us
    ppermute x1, waiting for transfers between devices, local(): wave = lax.ppermute(wave, 'depth', [(0, 1)])  6.08 us
  transfers between devices with their start and end apart: 23, of which 12 were waited for; matrix products, arithmetic and copies ran while one was open for 2% of the time, Pallas kernels for 3%

commit v1 on v0

--- a/solution.py
+++ b/solution.py
@@ -13,6 +13,7 @@
 WIN = 128
 HALF = 64
 TALL = WIN + 8
+LEAD = 4
 F32 = jnp.float32
 BF16 = jnp.bfloat16
 VMEM_LIMIT = 16 * 1024 * 1024
@@ -46,9 +47,20 @@
 
 def constants():
     prop, exit_left, exit_right = tables()
-    steps = np.stack([halves(right_block(prop)), halves(left_block(prop))])
+    steps = halves(right_block(prop))
     exits = np.stack([halves(right_block(exit_right)), halves(left_block(exit_left))])
     return jnp.asarray(steps), jnp.asarray(exits)
+
+
+def step_pair(mats):
+    right = (mats[0], mats[1])
+
+    def other(m):
+        top = jnp.concatenate([m[:WIN, :WIN], m[WIN:, :WIN]], axis=1)
+        bottom = jnp.concatenate([m[:WIN, WIN:], m[WIN:, WIN:]], axis=1)
+        return jnp.concatenate([top, bottom], axis=0)
+
+    return right, (other(right[0]), other(right[1]))
 
 
 def split(x):
@@ -61,7 +73,7 @@
 
 
 def mm3(a, b):
-    return mm(a[0], b[0]) + (mm(a[1], b[0]) + mm(a[0], b[1]))
+    return mm(jnp.concatenate([a[0], a[1], a[0]], axis=1), jnp.concatenate([b[0], b[0], b[1]], axis=0))
 
 
 def apply_both(fields, right, left):
@@ -133,16 +145,21 @@
     low = pos[2] * 64
     for out, start in ((first, 64 - low), (second, low)):
         rows = pl.ds(pl.multiple_of(start, 64), 64)
+        ring = inside(pos, col2[:, rows, :])
 
         @pl.when(even)
         def _():
-            out[:, :, :128] = col2[:, rows, :]
+            out[:, :, :128] = ring
             out[:, :, 128:] = col1[:, rows, :]
 
         @pl.when(jnp.logical_not(even))
         def _():
             out[:, :, :128] = col1[:, rows, :]
-            out[:, :, 128:] = col2[:, rows, :]
+            out[:, :, 128:] = ring
+
+
+def inside(pos, value):
+    return jnp.where(pos[3] == 1, 0.0, value)
 
 
 def load_window(ext, c, k, row, block, shift):
@@ -153,31 +170,26 @@
 
 
 def place(pos, p):
-    row = pos[3 + 2 * p] + HALF
-    col = pos[4 + 2 * p] + 128
+    row = pos[LEAD + 2 * p] + HALF
+    col = pos[LEAD + 1 + 2 * p] + 128
     return row, col // 128, col % 128
 
 
-def forward_kernel(
-    count, pos, probe_h, tile, col1_h, col2_h, row1, row2, crn1_h, crn2_h, mats_h,
-    wave, win, psi_h, ext, probe, mats, psi, cols, corners, sems,
-):
-    slabs = tile.shape[1]
+def assemble(pos, tile, cols_h, rows_h, corners_h, ext, cols, corners, sems):
     odd_row = pos[2]
     starts = (pl.multiple_of(192 * (1 - odd_row), 64), pl.multiple_of(192 * odd_row, 64))
     first = pos[1]
     near = [
-        fetch(col1_h, cols.at[1 - first], sems.at[0]),
-        fetch(col2_h, cols.at[first], sems.at[1]),
-        fetch(crn1_h, corners.at[0], sems.at[2]),
-        fetch(crn2_h, corners.at[1], sems.at[3]),
+        fetch(cols_h[0], cols.at[1 - first], sems.at[0]),
+        fetch(cols_h[1], cols.at[first], sems.at[1]),
+        fetch(corners_h[0], corners.at[0], sems.at[2]),
+        fetch(corners_h[1], corners.at[1], sems.at[3]),
     ]
     far = [
         fetch(tile, ext.at[:, :, pl.ds(64, 128), pl.ds(128, 256)], sems.at[4]),
-        fetch(row1, ext.at[:, :, pl.ds(starts[0], 64), pl.ds(128, 256)], sems.at[5]),
-        fetch(row2, ext.at[:, :, pl.ds(starts[1], 64), pl.ds(128, 256)], sems.at[6]),
+        fetch(rows_h[0], ext.at[:, :, pl.ds(starts[0], 64), pl.ds(128, 256)], sems.at[5]),
+        fetch(rows_h[1], ext.at[:, :, pl.ds(starts[1], 64), pl.ds(128, 256)], sems.at[6]),
     ]
-    loads = [fetch(probe_h, probe, sems.at[7]), fetch(mats_h, mats, sems.at[8])]
     for copy in near:
         copy.wait()
 
@@ -187,35 +199,81 @@
         ext[0, :, rows, 384:512] = right
         ext[1, :, rows, 384:512] = roll_half(right)
 
+    cols[first] = inside(pos, cols[first])
     sides(slice(64, 192), cols[0], cols[1])
     for i in range(2):
         sides(pl.ds(starts[i], 64), corners[i, :, :, :128], corners[i, :, :, 128:])
     for copy in far:
         copy.wait()
-    for copy in loads:
+
+
+def cut_window(pos, ext, p, k, win):
+    row, block, shift = place(pos, p)
+    win[k, p, 0] = load_window(ext, 0, k, row, block, shift) + 1.0
+    win[k, p, 1] = load_window(ext, 1, k, row, block, shift)
+
+
+def run_forward(span, probe, mats, win, wave, psi_h, psi, sems, after):
+    slabs = win.shape[0]
+    right, left = step_pair(mats)
+    fields = [(probe[0], probe[1])] * len(span)
+    saves = []
+    for k in range(slabs):
+        if k:
+            for i in range(len(span)):
+                psi[k - 1, i, 0], psi[k - 1, i, 1] = fields[i]
+            saves.append(fetch(psi.at[k - 1], psi_h.at[k - 1], sems.at[8 + k]))
+        fields = apply_both([times(fields[i], pair(win.at[k], p)) for i, p in enumerate(span)], right, left)
+        after(k)
+    for i in range(len(span)):
+        wave[i, 0], wave[i, 1] = fields[i]
+    for copy in saves:
         copy.wait()
-    for p in range(count):
-        row, block, shift = place(pos, p)
+
+
+def forward_first_kernel(
+    spans, pos, probe_h, tile, col1_h, col2_h, row1, row2, crn1_h, crn2_h, mats_h,
+    wave, win, psi_h, ext, probe, mats, psi, cols, corners, sems,
+):
+    slabs = tile.shape[1]
+
+    @pl.when(pos[0] == 0)
+    def _():
+        loads = [fetch(probe_h, probe, sems.at[7]), fetch(mats_h, mats, sems.at[8])]
+        assemble(pos, tile, (col1_h, col2_h), (row1, row2), (crn1_h, crn2_h), ext, cols, corners, sems)
+        for copy in loads:
+            copy.wait()
         for k in range(slabs):
-            win[k, p, 0] = load_window(ext, 0, k, row, block, shift) + 1.0
-            win[k, p, 1] = load_window(ext, 1, k, row, block, shift)
-
+            for p in spans[0]:
+                cut_window(pos, ext, p, k, win)
+
+        def after(k):
+            for p in spans[1]:
+                cut_window(pos, ext, p, k, win)
+
+        run_forward(spans[0], probe, mats, win, wave, psi_h, psi, sems, after)
+
+
+def forward_second_kernel(spans, pos, probe_h, win, mats_h, wave, psi_h, probe, mats, psi, sems):
     @pl.when(pos[0] == 0)
     def _():
-        right = (mats[0, 0], mats[0, 1])
-        left = (mats[1, 0], mats[1, 1])
-        fields = [(probe[0], probe[1])] * count
-        saves = []
-        for k in range(slabs):
-            if k:
-                for p in range(count):
-                    psi[k - 1, p, 0], psi[k - 1, p, 1] = fields[p]
-                saves.append(fetch(psi.at[k - 1], psi_h.at[k - 1], sems.at[8 + k]))
-            fields = apply_both([times(fields[p], pair(win.at[k], p)) for p in range(count)], right, left)
-        for p in range(count):
-            wave[p, 0], wave[p, 1] = fields[p]
-        for copy in saves:
+        loads = [fetch(probe_h, probe, sems.at[7]), fetch(mats_h, mats, sems.at[8])]
+        for copy in loads:
             copy.wait()
+        run_forward(spans[1], probe, mats, win, wave, psi_h, psi, sems, lambda k: None)
+
+
+def cut_kernel(count, pos, tile, col1_h, col2_h, row1, row2, crn1_h, crn2_h, win, ext, cols, corners, sems):
+    slabs = tile.shape[1]
+
+    @pl.when(pos[0] == 1)
+    def _():
+        assemble(pos, tile, (col1_h, col2_h), (row1, row2), (crn1_h, crn2_h), ext, cols, corners, sems)
+
+        @pl.loop(0, count)
+        def _(p):
+            for k in range(slabs):
+                cut_window(pos, ext, p, k, win)
 
 
 def add_window(ext, c, k, row, block, shift, piece):
@@ -244,7 +302,7 @@
     rim(second, 192 * odd_row)
 
 
-def backward_slabs(count, pos, grads, win, incident, ext, right, left, ext_h, sems):
+def backward_slabs(span, pos, grads, win, incident, ext, right, left, ext_h, sems, loads):
     slabs = win.shape[0]
     saves = []
     for k in reversed(range(slabs)):
@@ -252,22 +310,33 @@
             fields = grads[1]
         else:
             fields = apply_both(grads[1], left, right)
+        if loads:
+            loads[k].wait()
         nxt = []
-        for p in range(count):
+        for i, p in enumerate(span):
             row, block, shift = place(pos, p)
-            piece = conj_times(incident(k, p), fields[p])
+            piece = conj_times(incident(k, i), fields[i])
             add_window(ext, 0, k, row, block, shift, piece[0])
             add_window(ext, 1, k, row, block, shift, piece[1])
-            nxt.append(conj_times(pair(win.at[k], p), fields[p]))
+            nxt.append(conj_times(pair(win.at[k], p), fields[i]))
         saves.append(fetch(ext.at[:, k], ext_h.at[:, k], sems.at[k]))
         grads = ("inner", nxt)
     return grads[1], saves
 
 
-def middle_kernel(
-    count, pos, wave, win, measured_h, mats_h, exits_h, grad, error, ext_h, ext, psi, measured, mats, exits, sems
+def start_ext(group, ext, held_h, sems, at, slabs):
+    if group == 0:
+        ext[...] = jnp.zeros_like(ext)
+        return None
+    return [fetch(held_h.at[:, k], ext.at[:, k], sems.at[at + k]) for k in range(slabs)]
+
+
+def middle_body(
+    group, count, span, pos, wave, win, measured_h, mats_h, exits_h, held_h, before,
+    grad, error, ext_h, ext, psi, measured, mats, exits, sems,
 ):
     slabs = win.shape[0]
+    extra = slabs + 3
 
     @pl.when(pos[0] == 0)
     def _():
@@ -278,55 +347,97 @@
         loads = [
             fetch(mats_h, mats, sems.at[slabs]),
             fetch(exits_h, exits, sems.at[slabs + 1]),
-            fetch(measured_h, measured, sems.at[slabs + 2]),
+            fetch(measured_h.at[pl.ds(span[0], len(span))], measured, sems.at[slabs + 2]),
         ]
-        ext[...] = jnp.zeros_like(ext)
+        held = start_ext(group, ext, held_h, sems, extra, slabs)
         for copy in loads:
             copy.wait()
-        right = (mats[0, 0], mats[0, 1])
-        left = (mats[1, 0], mats[1, 1])
+        right, left = step_pair(mats)
         exit_right = (exits[0, 0], exits[0, 1])
         exit_left = (exits[1, 0], exits[1, 1])
-        fields = [pair(wave, p) for p in range(count)]
+        fields = [pair(wave, i) for i in range(len(span))]
         for k in range(slabs):
             if k:
-                for p in range(count):
-                    psi[k - 1, p, 0], psi[k - 1, p, 1] = fields[p]
-            entering = [times(fields[p], pair(win.at[k], p)) for p in range(count)]
+                for i in range(len(span)):
+                    psi[k - 1, i, 0], psi[k - 1, i, 1] = fields[i]
+            entering = [times(fields[i], pair(win.at[k], p)) for i, p in enumerate(span)]
             if k < slabs - 1:
                 fields = apply_both(entering, right, left)
             else:
                 fields = apply_both(entering, exit_right, exit_left)
         total = jnp.zeros((8, 128), F32)
         far = []
-        for p in range(count):
-            at = 3 + 2 * count + 2 * p
-            target = pltpu.roll(measured[p], (128 - pos[at]) & 127, axis=0)
+        for i, p in enumerate(span):
+            at = LEAD + 2 * count + 2 * p
+            target = pltpu.roll(measured[i], (128 - pos[at]) & 127, axis=0)
             target = pltpu.roll(target, (128 - pos[at + 1]) & 127, axis=1)
-            re, im = fields[p]
+            re, im = fields[i]
             residual = re * re + im * im - target
             total = total + jnp.sum((residual * residual).reshape(16, 8, 128), axis=0)
             twice = 2.0 * residual
             far.append((twice * re, twice * im))
-        error[...] = jnp.full((8, 128), 0.5 * jnp.sum(total), F32)
+        part = jnp.full((8, 128), 0.5 * jnp.sum(total), F32)
+        error[...] = part if group == 0 else before[...] + part
         entry = apply_both(far, exit_left, exit_right)
 
-        def incident(k, p):
-            return pair(wave, p) if k == 0 else pair(psi.at[k - 1], p)
-
-        out, saves = backward_slabs(count, pos, ("exit", entry), win, incident, ext, right, left, ext_h, sems)
-        for p in range(count):
-            grad[p, 0], grad[p, 1] = out[p]
+        def incident(k, i):
+            return pair(wave, i) if k == 0 else pair(psi.at[k - 1], i)
+
+        out, saves = backward_slabs(span, pos, ("exit", entry), win, incident, ext, right, left, ext_h, sems, held)
+        for i in range(len(span)):
+            grad[i, 0], grad[i, 1] = out[i]
         for copy in saves:
             copy.wait()
 
 
-def backward_kernel(
-    count, pos, grad, win, psi_h, probe_h, mats_h, ext1_h, error,
+def middle_first_kernel(count, span, pos, wave, win, measured_h, mats_h, exits_h, *rest):
+    middle_body(0, count, span, pos, wave, win, measured_h, mats_h, exits_h, None, None, *rest)
+
+
+def middle_second_kernel(count, span, pos, wave, win, measured_h, mats_h, exits_h, held_h, before, *rest):
+    middle_body(1, count, span, pos, wave, win, measured_h, mats_h, exits_h, held_h, before, *rest)
+
+
+def run_backward(group, span, pos, grad, win, psi_h, probe_h, mats_h, held_h, ext_h, ext, probe, mats, psi, sems):
+    slabs = win.shape[0]
+    loads = [
+        fetch(mats_h, mats, sems.at[slabs]),
+        fetch(psi_h, psi, sems.at[slabs + 1]),
+        fetch(probe_h, probe, sems.at[slabs + 2]),
+    ]
+    held = start_ext(group, ext, held_h, sems, slabs + 3, slabs)
+    for copy in loads:
+        copy.wait()
+    right, left = step_pair(mats)
+
+    def incident(k, i):
+        return (probe[0], probe[1]) if k == 0 else pair(psi.at[k - 1], i)
+
+    grads = ("inner", [pair(grad, i) for i in range(len(span))])
+    out, saves = backward_slabs(span, pos, grads, win, incident, ext, right, left, ext_h, sems, held)
+    re = sum(o[0] for o in out[1:]) + out[0][0]
+    im = sum(o[1] for o in out[1:]) + out[0][1]
+    return re, im, saves
+
+
+def backward_first_kernel(
+    span, pos, grad, win, psi_h, probe_h, mats_h, held_h, total, ext_h, ext, probe, mats, psi, sems
+):
+    @pl.when(pos[0] == 0)
+    def _():
+        re, im, saves = run_backward(
+            0, span, pos, grad, win, psi_h, probe_h, mats_h, held_h, ext_h, ext, probe, mats, psi, sems
+        )
+        total[0] = re
+        total[1] = im
+        for copy in saves:
+            copy.wait()
+
+
+def backward_second_kernel(
+    span, pos, grad, win, psi_h, probe_h, mats_h, held_h, error, total,
     keep, send, ext_h, first, second, ext, probe, mats, psi, sems,
 ):
-    slabs = win.shape[0]
-
     def packet(re, im):
         upper = jnp.concatenate([im[8:], error[...]], axis=0)
         lower = jnp.concatenate([re, im[:8]], axis=0)
@@ -345,7 +456,7 @@
 
     @pl.when(pos[0] == 1)
     def _():
-        load = fetch(ext1_h, ext, sems.at[0])
+        load = fetch(held_h, ext, sems.at[0])
         zero = jnp.zeros((WIN, WIN), F32)
         packet(zero, zero)
         load.wait()
@@ -353,23 +464,10 @@
 
     @pl.when(pos[0] == 0)
     def _():
-        loads = [
-            fetch(mats_h, mats, sems.at[slabs]),
-            fetch(psi_h, psi, sems.at[slabs + 1]),
-            fetch(probe_h, probe, sems.at[slabs + 2]),
-        ]
-        ext[...] = jnp.zeros_like(ext)
-        for copy in loads:
-            copy.wait()
-        right = (mats[0, 0], mats[0, 1])
-        left = (mats[1, 0], mats[1, 1])
-
-        def incident(k, p):
-            return (probe[0], probe[1]) if k == 0 else pair(psi.at[k - 1], p)
-
-        grads = ("inner", [pair(grad, p) for p in range(count)])
-        out, saves = backward_slabs(count, pos, grads, win, incident, ext, right, left, ext_h, sems)
-        packet(sum(o[0] for o in out[1:]) + out[0][0], sum(o[1] for o in out[1:]) + out[0][1])
+        re, im, saves = run_backward(
+            1, span, pos, grad, win, psi_h, probe_h, mats_h, held_h, ext_h, ext, probe, mats, psi, sems
+        )
+        packet(re + total[0], im + total[1])
         emit_rims(pos, ext, first, second)
         for copy in saves:
             copy.wait()
@@ -415,18 +513,18 @@
 
     def columns(from_left, from_right):
         zero = jnp.zeros(from_left.shape, F32)
-        out[0, :, :, :128] = out[0, :, :, :128] + join(from_left[...], zero)
-        out[1, :, :, :128] = out[1, :, :, :128] + join(roll_half(from_left[...]), zero)
-        out[0, :, :, 128:] = out[0, :, :, 128:] + join(zero, roll_half(from_right[...]))
-        out[1, :, :, 128:] = out[1, :, :, 128:] + join(zero, from_right[...])
+        out[0, :, :, :128] = out[0, :, :, :128] + join(from_left, zero)
+        out[1, :, :, :128] = out[1, :, :, :128] + join(roll_half(from_left), zero)
+        out[0, :, :, 128:] = out[0, :, :, 128:] + join(zero, roll_half(from_right))
+        out[1, :, :, 128:] = out[1, :, :, 128:] + join(zero, from_right)
 
     @pl.when(even)
     def _():
-        columns(col2, col1)
+        columns(inside(pos, col2[...]), col1[...])
 
     @pl.when(jnp.logical_not(even))
     def _():
-        columns(col1, col2)
+        columns(col1[...], inside(pos, col2[...]))
 
 
 def finish_kernel(scales, pos, keep, back, probe, error):
@@ -469,10 +567,19 @@
     )(*scalars, *arrays)
 
 
-def swap(value, axis, odd=False):
+def swap(value, axis):
+    pairs = [(i, i ^ 1) for i in range(lax.axis_size(axis))]
+    return lax.ppermute(value, axis, pairs)
+
+
+def swap_odd_ring(value, axis):
     size = lax.axis_size(axis)
-    pairs = [(i, ((i - 1) ^ 1) + 1) for i in range(1, size - 1)] if odd else [(i, i ^ 1) for i in range(size)]
-    return lax.ppermute(value, axis, pairs)
+    return lax.ppermute(value, axis, [(i, (((i - 1) % size) ^ 1) + 1 if i not in (0, size - 1) else size - 1 - i) for i in range(size)])
+
+
+def swap_odd(value, axis):
+    size = lax.axis_size(axis)
+    return lax.ppermute(value, axis, [(i, ((i - 1) ^ 1) + 1) for i in range(1, size - 1)])
 
 
 AXES = ("sx", "sy", "depth")
@@ -512,7 +619,9 @@
     measured = patterns.reshape(count, WIN, WIN)
     steps, exits = constants()
     core = lax.axis_index("sx") % 2
-    where = jnp.stack([lax.axis_index("depth"), lax.axis_index("sy") % 2, core]).astype(jnp.int32)
+    column = lax.axis_index("sy")
+    edge_column = (column == 0) | (column == lax.axis_size("sy") - 1)
+    where = jnp.stack([lax.axis_index("depth"), column % 2, core, edge_column.astype(jnp.int32)]).astype(jnp.int32)
     pos = jnp.concatenate([where, scan_offsets.reshape(-1), pattern_shifts.reshape(-1)])
     sizes = (lax.axis_size("sx"), lax.axis_size("sy"), lax.axis_size("depth"))
 
@@ -521,10 +630,10 @@
     rim = (slabs, HALF, 768)
     side = (2, slabs, HALF, cols)
     corner = (slabs, HALF, 256)
-    field = (count, 2, WIN, WIN)
+    field = (count // 2, 2, WIN, WIN)
     inner = (slabs - 1,) + field
     ext = (2, slabs, rows + 2 * HALF + 8, 512)
-    step_flops = 2 * 3 * 2 * 256 * 256 * WIN * count
+    step_flops = 3 * 2 * 256 * 256 * WIN * count
 
     def vmem(shape, dtype=F32):
         return pltpu.VMEM(shape, dtype)
@@ -538,47 +647,98 @@
     col1, col2, row1, row2 = call(
         pack_kernel, [strip, strip, side, side], [where], [transmission], [vmem(tile), sems(1)], hbm=(0,), fixed=(0,)
     )
-    col1, col2 = swap(col1, "sy"), swap(col2, "sy", True)
-    row1, row2 = swap(row1, "sx"), swap(row2, "sx", True)
+    col1, col2 = swap(col1, "sy"), swap_odd_ring(col2, "sy")
+    row1, row2 = swap(row1, "sx"), swap_odd(row2, "sx")
     crn1, crn2 = call(pack_corners_kernel, [corner, corner], [where], [col1, col2])
-    crn1, crn2 = swap(crn1, "sx"), swap(crn2, "sx", True)
-    wave, win, psi = call(
-        functools.partial(forward_kernel, count),
-        [field, (slabs,) + field, inner],
+    crn1, crn2 = swap(crn1, "sx"), swap_odd(crn2, "sx")
+    spans = (tuple(range(count // 2)), tuple(range(count // 2, count)))
+    assembly = [vmem(ext)]
+    parts = [vmem((2,) + strip), vmem((2,) + corner)]
+    wave_a, win, psi_a = call(
+        functools.partial(forward_first_kernel, spans),
+        [field, (slabs, count, 2, WIN, WIN), inner],
         [pos],
         [probe_wave, transmission, col1, col2, row1, row2, crn1, crn2, steps],
-        [vmem(ext), probe, mats, vmem(inner), vmem((2,) + strip), vmem((2,) + corner), sems(slabs + 8)],
+        [vmem(ext), probe, mats, vmem(inner)] + parts + [sems(slabs + 8)],
         slabs * step_flops,
         hbm=tuple(range(9)),
+        hbm_out=(2,),
         fixed=(0, 1, 8),
-        hbm_out=(2,),
-    )
-    wave = lax.ppermute(wave, "depth", [(0, 1)])
-    grad, error, edge = call(
-        functools.partial(middle_kernel, count),
+    )
+    wave_a = lax.ppermute(wave_a, "depth", [(0, 1)])
+    wave_b, psi_b = call(
+        functools.partial(forward_second_kernel, spans),
+        [field, inner],
+        [pos],
+        [probe_wave, win, steps],
+        [probe, mats, vmem(inner), sems(slabs + 8)],
+        slabs * step_flops,
+        hbm=(0, 2),
+        hbm_out=(1,),
+        fixed=(0, 2),
+    )
+    wave_b = lax.ppermute(wave_b, "depth", [(0, 1)])
+    (win1,) = call(
+        functools.partial(cut_kernel, count),
+        [(slabs, count, 2, WIN, WIN)],
+        [pos],
+        [transmission, col1, col2, row1, row2, crn1, crn2],
+        assembly + parts + [sems(7)],
+        0,
+        hbm=tuple(range(7)),
+        fixed=(0,),
+    )
+    half = (len(spans[0]), WIN, WIN)
+    grad_a, error, edge = call(
+        functools.partial(middle_first_kernel, count, spans[0]),
         [field, (8, 128), ext],
         [pos],
-        [wave, win, measured, steps, exits],
-        [vmem(ext), vmem(inner), vmem(measured.shape), mats, mats, sems(slabs + 3)],
+        [wave_a, win1, measured, steps, exits],
+        [vmem(ext), vmem(inner), vmem(half), mats, vmem(exits.shape, BF16), sems(slabs + 3)],
         2 * slabs * step_flops,
         hbm=(2, 3, 4),
+        hbm_out=(2,),
         fixed=(2, 3, 4),
+    )
+    grad_a = lax.ppermute(grad_a, "depth", [(1, 0)])
+    grad_b, error, edge = call(
+        functools.partial(middle_second_kernel, count, spans[1]),
+        [field, (8, 128), ext],
+        [pos],
+        [wave_b, win1, measured, steps, exits, edge, error],
+        [vmem(ext), vmem(inner), vmem(half), mats, vmem(exits.shape, BF16), sems(2 * slabs + 3)],
+        2 * slabs * step_flops,
+        hbm=(2, 3, 4, 5),
         hbm_out=(2,),
-    )
-    grad = lax.ppermute(grad, "depth", [(1, 0)])
-    part, other, edge, row1, row2 = call(
-        functools.partial(backward_kernel, count),
-        [(136, WIN), (136, WIN), ext, rim, rim],
+        fixed=(2, 3, 4),
+        aliases={6: 2},
+    )
+    grad_b = lax.ppermute(grad_b, "depth", [(1, 0)])
+    total, edge = call(
+        functools.partial(backward_first_kernel, spans[0]),
+        [(2, WIN, WIN), ext],
         [pos],
-        [grad, win, psi, probe_wave, steps, edge, error],
+        [grad_a, win, psi_a, probe_wave, steps, edge],
         [vmem(ext), probe, mats, vmem(inner), sems(slabs + 3)],
         slabs * step_flops,
         hbm=(2, 3, 4, 5),
+        hbm_out=(1,),
         fixed=(3, 4),
+        aliases={6: 1},
+    )
+    part, other, edge, row1, row2 = call(
+        functools.partial(backward_second_kernel, spans[1]),
+        [(136, WIN), (136, WIN), ext, rim, rim],
+        [pos],
+        [grad_b, win, psi_b, probe_wave, steps, edge, error, total],
+        [vmem(ext), probe, mats, vmem(inner), sems(2 * slabs + 3)],
+        slabs * step_flops,
+        hbm=(2, 3, 4, 5),
         hbm_out=(2,),
+        fixed=(3, 4),
         aliases={6: 2},
     )
-    row1, row2 = swap(row1, "sx"), swap(row2, "sx", True)
+    row1, row2 = swap(row1, "sx"), swap_odd(row2, "sx")
     part = part + swap(other, "sx")
     part = ring_sum(part, sizes, turn_x)
     part, row1, row2 = lax.optimization_barrier((part, row1, row2))
@@ -587,7 +747,7 @@
         [vmem((2, 2) + strip), sems(2)], hbm=(0,),
     )
     part, col1, col2 = lax.optimization_barrier((part, col1, col2))
-    col1, col2 = swap(col1, "sy"), swap(col2, "sy", True)
+    col1, col2 = swap(col1, "sy"), swap_odd_ring(col2, "sy")
     part = ring_sum(part, sizes, turn_z)
     part, col1, col2 = lax.optimization_barrier((part, col1, col2))
     (out,) = call(fold_kernel, [tile], [where], [edge, row1, row2, col1, col2], [sems(1)], hbm=(0,))

time: 119 us -> 117 us (0.983)
  the two profiles are of different devices: /device:TPU:33 before, /device:TPU:1 now
where the time goes in v1:
time: 117 us; the launch traced here: 116 us
  starting transfers between devices  45.6 us (39%)
  waiting for transfers between devices  36.6 us (31%)
  Pallas kernels  31 us (26%)
  local copies, waits for them, and re-layouts  1.79 us (2%)
    pallas_call x12, Pallas kernels, call(): pl.pallas_call(kernel, out_shape=outs, in_specs=[pl.BlockSpec(memory_spac...  31 us
    ppermute x3, starting transfers between devices, swap_odd(): lax.ppermute(value, axis, [(i, (i - 1 ^ 1) + 1) for i in range(1, size -...  15.5 us
    ppermute x1, waiting for transfers between devices, local(): grad_a = lax.ppermute(grad_a, 'depth', [(1, 0)])  10.2 us
    ppermute x9, waiting for transfers between devices, ring_sum(): got.append(lax.ppermute(value, AXES, pairs))  10 us
    ppermute x7, starting transfers between devices, swap(): return lax.ppermute(value, axis, pairs)  8.81 us
    ppermute x2, starting transfers between devices, swap_odd_ring(): lax.ppermute(value, axis, [(i, ((i - 1) % size ^ 1) + 1 if i not in (0, s...  8.41 us
    ppermute x9, starting transfers between devices, ring_sum(): got.append(lax.ppermute(value, AXES, pairs))  7.72 us
    ppermute x3, waiting for transfers between devices, swap_odd(): lax.ppermute(value, axis, [(i, (i - 1 ^ 1) + 1) for i in range(1, size -...  4.76 us
  transfers between devices with their start and end apart: 25, of which 15 were waited for; matrix products, arithmetic and copies ran while one was open for 2% of the time, Pallas kernels for 13%

profile of v1, /device:TPU:1, one launch (start us, length us, event | category | flops | bytes accessed | tf_op | source)
XLA Modules:
  0.0 116.3 jit_solution(5974289415584746771)
XLA Ops:
  0.7 2.1 %shard_map.103 = (f32[4,128,128]{2,1,0:T(8,128)S(1)}, f32[4,128,128]{2,1,0:T(8,128)S(1)}, f32[2,4,64,256]{3,2,1,0:T(8,128)S(1)}, f32[2,4,64,256]{3,2,1,0:T(8,128)S(1)}) custom-call(s32[4]{0:T(128)S(1)} %pad_add_fusion.pos, f32[2,4,128,256]{3,2,1,0:T(8,128)} %tile.3), custom_call_target="tpu_custom_call" | custom-call | bytes 2621440 | tf_op jit(solution)/shard_map/pallas_call | solution.py:554
  2.8 2.1 %collective-permute-start = (f32[4,128,128]{2,1,0:T(8,128)S(1)}, f32[4,128,128]{2,1,0:T(8,128)S(1)}, u32[]{:S(2)}, u32[]{:S(2)}) collective-permute-start(f32[4,128,128]{2,1,0:T(8,128)S(1)} %get-tuple-element.40), channel_id=1, source_target_pairs={{0,2},{2,0},{4,6},{6,4},{8,10},{10,8},{12,14},{14,12},{16,18},{18,... | collective-permute-start | bytes 786440 | tf_op jit(solution)/shard_map/ppermute | solution.py:572
  4.9 5.3 %collective-permute-start.1 = (f32[4,128,128]{2,1,0:T(8,128)S(1)}, f32[4,128,128]{2,1,0:T(8,128)S(1)}, u32[]{:S(2)}, u32[]{:S(2)}) collective-permute-start(f32[4,128,128]{2,1,0:T(8,128)S(1)} %get-tuple-element.41), channel_id=1, source_target_pairs={{0,30},{2,4},{4,2},{6,8},{8,6},{10,12},{12,10},{14,16},{16,14},{18... | collective-permute-start | bytes 786440 | tf_op jit(solution)/shard_map/ppermute | solution.py:577
  11.5 4.7 %collective-permute-start.3 = (f32[2,4,64,256]{3,2,1,0:T(8,128)S(1)}, f32[2,4,64,256]{3,2,1,0:T(8,128)S(1)}, u32[]{:S(2)}, u32[]{:S(2)}) collective-permute-start(f32[2,4,64,256]{3,2,1,0:T(8,128)S(1)} %get-tuple-element.43), channel_id=1, source_target_pairs={{32,64},{64,32},{33,65},{65,33},{34,66},{66,34},{35,67},{67,35},{3... | collective-permute-start | bytes 1572872 | tf_op jit(solution)/shard_map/ppermute | solution.py:582
  18.8 4.7 %collective-permute-start.5 = (f32[4,64,256]{2,1,0:T(8,128)S(1)}, f32[4,64,256]{2,1,0:T(8,128)S(1)}, u32[]{:S(2)}, u32[]{:S(2)}) collective-permute-start(f32[4,64,256]{2,1,0:T(8,128)S(1)} %get-tuple-element.45), channel_id=1, source_target_pairs={{32,64},{64,32},{33,65},{65,33},{34,66},{66,34},{35,67},{67,35},{3... | collective-permute-start | bytes 786440 | tf_op jit(solution)/shard_map/ppermute | solution.py:582
  25.3 2.7 %collective-permute-done.5.crn2_h = f32[4,64,256]{2,1,0:T(8,128)S(1)} collective-permute-done((f32[4,64,256]{2,1,0:T(8,128)S(1)}, f32[4,64,256]{2,1,0:T(8,128)S(1)}, u32[]{:S(2)}, u32[]{:S(2)}) %collective-permute-start.5) | collective-permute-done | bytes 262176 | tf_op jit(solution)/shard_map/ppermute | solution.py:582
  28.0 5.1 %shard_map.105 = (f32[2,2,128,128]{3,2,1,0:T(8,128)S(1)}, f32[4,4,2,128,128]{4,3,2,1,0:T(8,128)S(1)}, f32[3,2,2,128,128]{4,3,2,1,0:T(8,128)S(1)}) custom-call(s32[20]{0:T(128)S(1)} %concatenate.4.pos, f32[2,128,128]{2,1,0:T(8,128)} %probe_h.7, f32[2,4,128,256]{3,2,1,0:T(8,128)} %tile.3, f32[4,128,128]{2,1,0:T(8,128)S(1)} %collective-permute-done.col1.col1_h, ...), custom_call_target="tpu_custom_call" | custom-call | flops 805306368 | bytes 6946816 | tf_op jit(solution)/shard_map/pallas_call | solution.py:554
  34.4 4.5 %shard_map.106 = (f32[2,2,128,128]{3,2,1,0:T(8,128)S(1)}, f32[3,2,2,128,128]{4,3,2,1,0:T(8,128)S(1)}) custom-call(s32[20]{0:T(128)S(1)} %concatenate.4.pos, f32[2,128,128]{2,1,0:T(8,128)} %probe_h.7, f32[4,4,2,128,128]{4,3,2,1,0:T(8,128)S(1)} %get-tuple-element.46.win, bf16[2,256,256]{2,1,0:T(8,128)(2,1)} %constant.40.clone.mats_h), custom_call_target="tpu_custom_call" | custom-call | flops 805306368 | bytes 3801088 | tf_op jit(solution)/shard_map/pallas_call | solution.py:554
  45.6 10.2 %collective-permute-done.9.grad = f32[2,2,128,128]{3,2,1,0:T(8,128)S(1)} collective-permute-done((f32[2,2,128,128]{3,2,1,0:T(8,128)S(1)}, f32[2,2,128,128]{3,2,1,0:T(8,128)S(1)}, u32[]{:S(2)}, u32[]{:S(2)}) %collective-permute-start.9) | collective-permute-done | bytes 262176 | tf_op jit(solution)/shard_map/ppermute | solution.py:703
  55.8 5.5 %shard_map.110 = (f32[2,128,128]{2,1,0:T(8,128)S(1)}, f32[2,4,264,512]{3,2,1,0:T(8,128)S(1)}) custom-call(s32[20]{0:T(128)S(1)} %concatenate.4.pos, f32[2,2,128,128]{3,2,1,0:T(8,128)S(1)} %collective-permute-done.9.grad, f32[4,4,2,128,128]{4,3,2,1,0:T(8,128)S(1)} %get-tuple-element.46.win, ...), custom_call_target="tpu_custom_call", output_to_operand_aliasing={{1}: (6, {})} | custom-call | flops 805306368 | bytes 12582912 | tf_op jit(solution)/shard_map/pallas_call | solution.py:554
  61.3 3.7 %collective-permute-done.8.grad = f32[2,2,128,128]{3,2,1,0:T(8,128)S(1)} collective-permute-done((f32[2,2,128,128]{3,2,1,0:T(8,128)S(1)}, f32[2,2,128,128]{3,2,1,0:T(8,128)S(1)}, u32[]{:S(2)}, u32[]{:S(2)}) %collective-permute-start.8) | collective-permute-done | bytes 262176 | tf_op jit(solution)/shard_map/ppermute | solution.py:716
  64.9 6.0 %shard_map.111 = (f32[136,128]{1,0:T(8,128)S(1)}, f32[136,128]{1,0:T(8,128)S(1)}, f32[2,4,264,512]{3,2,1,0:T(8,128)S(1)}, f32[4,64,768]{2,1,0:T(8,128)S(1)}, f32[4,64,768]{2,1,0:T(8,128)S(1)}) custom-call(s32[20]{0:T(128)S(1)} %concatenate.4.pos, f32[2,2,128,128]{3,2,1,0:T(8,128)S(1)} %collective-permute-done.8.grad, ...), custom_call_target="tpu_custom_call", output_to_operand_aliasing={{2}: (6, {})} | custom-call | flops 805306368 | bytes 14299136 | tf_op jit(solution)/shard_map/pallas_call | solution.py:554
  71.0 6.1 %collective-permute-start.15 = (f32[4,64,768]{2,1,0:T(8,128)S(1)}, f32[4,64,768]{2,1,0:T(8,128)S(1)}, u32[]{:S(2)}, u32[]{:S(2)}) collective-permute-start(f32[4,64,768]{2,1,0:T(8,128)S(1)} %get-tuple-element.63), channel_id=1, source_target_pairs={{32,64},{64,32},{33,65},{65,33},{34,66},{66,34},{35,67},{67,35},{3... | collective-permute-start | bytes 2359304 | tf_op jit(solution)/shard_map/ppermute | solution.py:582
  80.0 2.1 %collective-permute-done.13 = f32[136,128]{1,0:T(8,128)S(1)} collective-permute-done((f32[136,128]{1,0:T(8,128)S(1)}, f32[136,128]{1,0:T(8,128)S(1)}, u32[]{:S(2)}, u32[]{:S(2)}) %collective-permute-start.13) | collective-permute-done | bytes 69664 | tf_op jit(solution)/shard_map/ppermute | solution.py:599
  83.0 1.7 %collective-permute-done.11 = f32[136,128]{1,0:T(8,128)S(1)} collective-permute-done((f32[136,128]{1,0:T(8,128)S(1)}, f32[136,128]{1,0:T(8,128)S(1)}, u32[]{:S(2)}, u32[]{:S(2)}) %collective-permute-start.11) | collective-permute-done | bytes 69664 | tf_op jit(solution)/shard_map/ppermute | solution.py:599
  84.7 2.1 %collective-permute-done.15.row2 = f32[4,64,768]{2,1,0:T(8,128)S(1)} collective-permute-done((f32[4,64,768]{2,1,0:T(8,128)S(1)}, f32[4,64,768]{2,1,0:T(8,128)S(1)}, u32[]{:S(2)}, u32[]{:S(2)}) %collective-permute-start.15) | collective-permute-done | bytes 786464 | tf_op jit(solution)/shard_map/ppermute | solution.py:582
  88.0 3.4 %collective-permute-start.18 = (f32[136,128]{1,0:T(8,128)S(1)}, f32[136,128]{1,0:T(8,128)S(1)}, u32[]{:S(2)}, u32[]{:S(2)}) collective-permute-start(f32[136,128]{1,0:T(8,128)S(1)} %add_add_fusion.2), channel_id=1, source_target_pairs={{0,24},{1,25},{2,26},{3,27},{4,28},{5,29},{6,30},{7,31},{8,0},{9,1... | collective-permute-start | bytes 208904 | tf_op jit(solution)/shard_map/ppermute | solution.py:599
  92.7 3.1 %collective-permute-start.20 = (f32[4,128,128]{2,1,0:T(8,128)S(1)}, f32[4,128,128]{2,1,0:T(8,128)S(1)}, u32[]{:S(2)}, u32[]{:S(2)}) collective-permute-start(f32[4,128,128]{2,1,0:T(8,128)S(1)} %get-tuple-element.71), channel_id=1, source_target_pairs={{0,30},{2,4},{4,2},{6,8},{8,6},{10,12},{12,10},{14,16},{16,14},{18... | collective-permute-start | bytes 786440 | tf_op jit(solution)/shard_map/ppermute | solution.py:577
  96.6 2.6 %collective-permute-done.19.col1 = f32[4,128,128]{2,1,0:T(8,128)S(1)} collective-permute-done((f32[4,128,128]{2,1,0:T(8,128)S(1)}, f32[4,128,128]{2,1,0:T(8,128)S(1)}, u32[]{:S(2)}, u32[]{:S(2)}) %collective-permute-start.19) | collective-permute-done | bytes 262176 | tf_op jit(solution)/shard_map/ppermute | solution.py:572
  99.2 3.3 %collective-permute-done.20.col2 = f32[4,128,128]{2,1,0:T(8,128)S(1)} collective-permute-done((f32[4,128,128]{2,1,0:T(8,128)S(1)}, f32[4,128,128]{2,1,0:T(8,128)S(1)}, u32[]{:S(2)}, u32[]{:S(2)}) %collective-permute-start.20) | collective-permute-done | bytes 262176 | tf_op jit(solution)/shard_map/ppermute | solution.py:577
  104.0 1.7 %collective-permute-done.23 = f32[136,128]{1,0:T(8,128)S(1)} collective-permute-done((f32[136,128]{1,0:T(8,128)S(1)}, f32[136,128]{1,0:T(8,128)S(1)}, u32[]{:S(2)}, u32[]{:S(2)}) %collective-permute-start.23) | collective-permute-done | bytes 69664 | tf_op jit(solution)/shard_map/ppermute | solution.py:599
  106.9 1.8 %collective-permute-done.21 = f32[136,128]{1,0:T(8,128)S(1)} collective-permute-done((f32[136,128]{1,0:T(8,128)S(1)}, f32[136,128]{1,0:T(8,128)S(1)}, u32[]{:S(2)}, u32[]{:S(2)}) %collective-permute-start.21) | collective-permute-done | bytes 69664 | tf_op jit(solution)/shard_map/ppermute | solution.py:599
  108.7 4.0 %collective-permute-start.24 = (f32[136,128]{1,0:T(8,128)S(1)}, f32[136,128]{1,0:T(8,128)S(1)}, u32[]{:S(2)}, u32[]{:S(2)}) collective-permute-start(f32[136,128]{1,0:T(8,128)S(1)} %add_add_fusion.keep), channel_id=1, source_target_pairs={{0,32},{32,0},{64,96},{96,64},{1,33},{33,1},{65,97},{97,65},{2,34}... | collective-permute-start | bytes 208904 | tf_op jit(solution)/shard_map/ppermute | solution.py:572
  112.7 2.0 %shard_map.113 = f32[2,4,128,256]{3,2,1,0:T(8,128)} custom-call(s32[4]{0:T(128)S(1)} %pad_add_fusion.pos, f32[2,4,264,512]{3,2,1,0:T(8,128)S(1)} %get-tuple-element.59.ext_h, f32[4,64,768]{2,1,0:T(8,128)S(1)} %collective-permute-done.14.row1, f32[4,64,768]{2,1,0:T(8,128)S(1)} %collective-permute-done.15.row2, ...), custom_call_target="tpu_custom_call" | custom-call | bytes 7471104 | tf_op jit(solution)/shard_map/pallas_call | solution.py:554
  (50 shorter events, 24.8 us)
Async XLA Ops:
  2.8 13.3 %collective-permute-start = (f32[4,128,128]{2,1,0:T(8,128)S(1)}, f32[4,128,128]{2,1,0:T(8,128)S(1)}, u32[]{:S(2)}, u32[]{:S(2)}) collective-permute-start(f32[4,128,128]{2,1,0:T(8,128)S(1)} %get-tuple-element.40), channel_id=1, source_target_pairs={{0,2},{2,0},{4,6},{6,4},{8,10},{10,8},{12,14},{14,12},{16,18},{18,... | collective-permute-start | bytes 786440 | tf_op jit(solution)/shard_map/ppermute | solution.py:572
  4.9 11.2 %collective-permute-start.1 = (f32[4,128,128]{2,1,0:T(8,128)S(1)}, f32[4,128,128]{2,1,0:T(8,128)S(1)}, u32[]{:S(2)}, u32[]{:S(2)}) collective-permute-start(f32[4,128,128]{2,1,0:T(8,128)S(1)} %get-tuple-element.41), channel_id=1, source_target_pairs={{0,30},{2,4},{4,2},{6,8},{8,6},{10,12},{12,10},{14,16},{16,14},{18... | collective-permute-start | bytes 786440 | tf_op jit(solution)/shard_map/ppermute | solution.py:577
  10.2 17.7 %collective-permute-start.2 = (f32[2,4,64,256]{3,2,1,0:T(8,128)S(1)}, f32[2,4,64,256]{3,2,1,0:T(8,128)S(1)}, u32[]{:S(2)}, u32[]{:S(2)}) collective-permute-start(f32[2,4,64,256]{3,2,1,0:T(8,128)S(1)} %get-tuple-element.42), channel_id=1, source_target_pairs={{0,32},{32,0},{64,96},{96,64},{1,33},{33,1},{65,97},{97,65},{2,34}... | collective-permute-start | bytes 1572872 | tf_op jit(solution)/shard_map/ppermute | solution.py:572
  11.5 16.5 %collective-permute-start.3 = (f32[2,4,64,256]{3,2,1,0:T(8,128)S(1)}, f32[2,4,64,256]{3,2,1,0:T(8,128)S(1)}, u32[]{:S(2)}, u32[]{:S(2)}) collective-permute-start(f32[2,4,64,256]{3,2,1,0:T(8,128)S(1)} %get-tuple-element.43), channel_id=1, source_target_pairs={{32,64},{64,32},{33,65},{65,33},{34,66},{66,34},{35,67},{67,35},{3... | collective-permute-start | bytes 1572872 | tf_op jit(solution)/shard_map/ppermute | solution.py:582
  17.5 7.8 %collective-permute-start.4 = (f32[4,64,256]{2,1,0:T(8,128)}, f32[4,64,256]{2,1,0:T(8,128)S(1)}, u32[]{:S(2)}, u32[]{:S(2)}) collective-permute-start(f32[4,64,256]{2,1,0:T(8,128)} %get-tuple-element.44), channel_id=1, source_target_pairs={{0,32},{32,0},{64,96},{96,64},{1,33},{33,1},{65,97},{97,65},{2,34}... | collective-permute-start | bytes 786440 | tf_op jit(solution)/shard_map/ppermute | solution.py:572
  18.8 9.2 %collective-permute-start.5 = (f32[4,64,256]{2,1,0:T(8,128)S(1)}, f32[4,64,256]{2,1,0:T(8,128)S(1)}, u32[]{:S(2)}, u32[]{:S(2)}) collective-permute-start(f32[4,64,256]{2,1,0:T(8,128)S(1)} %get-tuple-element.45), channel_id=1, source_target_pairs={{32,64},{64,32},{33,65},{65,33},{34,66},{66,34},{35,67},{67,35},{3... | collective-permute-start | bytes 786440 | tf_op jit(solution)/shard_map/ppermute | solution.py:582
  33.1 7.7 %collective-permute-start.7 = (f32[2,2,128,128]{3,2,1,0:T(8,128)S(1)}, f32[2,2,128,128]{3,2,1,0:T(8,128)S(1)}, u32[]{:S(2)}, u32[]{:S(2)}) collective-permute-start(f32[2,2,128,128]{3,2,1,0:T(8,128)S(1)} %get-tuple-element.48), channel_id=1, source_target_pairs={{0,1},{2,3},{4,5},{6,7},{8,9},{10,11},{12,13},{14,15},{16,17},{18,... | collective-permute-start | bytes 786440 | tf_op jit(solution)/shard_map/ppermute | solution.py:668
  38.9 4.6 %collective-permute-start.6 = (f32[2,2,128,128]{3,2,1,0:T(8,128)S(1)}, f32[2,2,128,128]{3,2,1,0:T(8,128)S(1)}, u32[]{:S(2)}, u32[]{:S(2)}) collective-permute-start(f32[2,2,128,128]{3,2,1,0:T(8,128)S(1)} %get-tuple-element.47), channel_id=1, source_target_pairs={{0,1},{2,3},{4,5},{6,7},{8,9},{10,11},{12,13},{14,15},{16,17},{18,... | collective-permute-start | bytes 786440 | tf_op jit(solution)/shard_map/ppermute | solution.py:680
  41.4 14.3 %collective-permute-start.9 = (f32[2,2,128,128]{3,2,1,0:T(8,128)S(1)}, f32[2,2,128,128]{3,2,1,0:T(8,128)S(1)}, u32[]{:S(2)}, u32[]{:S(2)}) collective-permute-start(f32[2,2,128,128]{3,2,1,0:T(8,128)S(1)} %get-tuple-element.53), channel_id=1, source_target_pairs={{1,0},{3,2},{5,4},{7,6},{9,8},{11,10},{13,12},{15,14},{17,16},{19,... | collective-permute-start | bytes 786440 | tf_op jit(solution)/shard_map/ppermute | solution.py:703
  44.3 20.6 %collective-permute-start.8 = (f32[2,2,128,128]{3,2,1,0:T(8,128)S(1)}, f32[2,2,128,128]{3,2,1,0:T(8,128)S(1)}, u32[]{:S(2)}, u32[]{:S(2)}) collective-permute-start(f32[2,2,128,128]{3,2,1,0:T(8,128)S(1)} %get-tuple-element.51), channel_id=1, source_target_pairs={{1,0},{3,2},{5,4},{7,6},{9,8},{11,10},{13,12},{15,14},{17,16},{19,... | collective-permute-start | bytes 786440 | tf_op jit(solution)/shard_map/ppermute | solution.py:716
  71.0 13.8 %collective-permute-start.14 = (f32[4,64,768]{2,1,0:T(8,128)S(1)}, f32[4,64,768]{2,1,0:T(8,128)S(1)}, u32[]{:S(2)}, u32[]{:S(2)}) collective-permute-start(f32[4,64,768]{2,1,0:T(8,128)S(1)} %get-tuple-element.62), channel_id=1, source_target_pairs={{0,32},{32,0},{64,96},{96,64},{1,33},{33,1},{65,97},{97,65},{2,34}... | collective-permute-start | bytes 2359304 | tf_op jit(solution)/shard_map/ppermute | solution.py:572
  71.0 15.7 %collective-permute-start.15 = (f32[4,64,768]{2,1,0:T(8,128)S(1)}, f32[4,64,768]{2,1,0:T(8,128)S(1)}, u32[]{:S(2)}, u32[]{:S(2)}) collective-permute-start(f32[4,64,768]{2,1,0:T(8,128)S(1)} %get-tuple-element.63), channel_id=1, source_target_pairs={{32,64},{64,32},{33,65},{65,33},{34,66},{66,34},{35,67},{67,35},{3... | collective-permute-start | bytes 2359304 | tf_op jit(solution)/shard_map/ppermute | solution.py:582
  78.5 3.6 %collective-permute-start.13 = (f32[136,128]{1,0:T(8,128)S(1)}, f32[136,128]{1,0:T(8,128)S(1)}, u32[]{:S(2)}, u32[]{:S(2)}) collective-permute-start(f32[136,128]{1,0:T(8,128)S(1)} %add.39), channel_id=1, source_target_pairs={{0,6},{1,7},{2,0},{3,1},{4,2},{5,3},{6,4},{7,5},{8,14},{9,15},{10,... | collective-permute-start | bytes 208904 | tf_op jit(solution)/shard_map/ppermute | solution.py:599
  78.7 4.4 %collective-permute-start.12 = (f32[136,128]{1,0:T(8,128)S(1)}, f32[136,128]{1,0:T(8,128)S(1)}, u32[]{:S(2)}, u32[]{:S(2)}) collective-permute-start(f32[136,128]{1,0:T(8,128)S(1)} %add.39), channel_id=1, source_target_pairs={{0,2},{1,3},{2,4},{3,5},{4,6},{5,7},{6,0},{7,1},{8,10},{9,11},{10,... | collective-permute-start | bytes 208904 | tf_op jit(solution)/shard_map/ppermute | solution.py:599
  80.0 4.7 %collective-permute-start.11 = (f32[136,128]{1,0:T(8,128)S(1)}, f32[136,128]{1,0:T(8,128)S(1)}, u32[]{:S(2)}, u32[]{:S(2)}) collective-permute-start(f32[136,128]{1,0:T(8,128)S(1)} %add.39), channel_id=1, source_target_pairs={{0,4},{1,5},{2,6},{3,7},{4,0},{5,1},{6,2},{7,3},{8,12},{9,13},{10,... | collective-permute-start | bytes 208904 | tf_op jit(solution)/shard_map/ppermute | solution.py:599
  88.0 7.8 %collective-permute-start.18 = (f32[136,128]{1,0:T(8,128)S(1)}, f32[136,128]{1,0:T(8,128)S(1)}, u32[]{:S(2)}, u32[]{:S(2)}) collective-permute-start(f32[136,128]{1,0:T(8,128)S(1)} %add_add_fusion.2), channel_id=1, source_target_pairs={{0,24},{1,25},{2,26},{3,27},{4,28},{5,29},{6,30},{7,31},{8,0},{9,1... | collective-permute-start | bytes 208904 | tf_op jit(solution)/shard_map/ppermute | solution.py:599
  91.5 5.1 %collective-permute-start.17 = (f32[136,128]{1,0:T(8,128)S(1)}, f32[136,128]{1,0:T(8,128)S(1)}, u32[]{:S(2)}, u32[]{:S(2)}) collective-permute-start(f32[136,128]{1,0:T(8,128)S(1)} %add_add_fusion.2), channel_id=1, source_target_pairs={{0,8},{1,9},{2,10},{3,11},{4,12},{5,13},{6,14},{7,15},{8,16},{9,17... | collective-permute-start | bytes 208904 | tf_op jit(solution)/shard_map/ppermute | solution.py:599
  91.5 5.1 %collective-permute-start.16 = (f32[136,128]{1,0:T(8,128)S(1)}, f32[136,128]{1,0:T(8,128)S(1)}, u32[]{:S(2)}, u32[]{:S(2)}) collective-permute-start(f32[136,128]{1,0:T(8,128)S(1)} %add_add_fusion.2), channel_id=1, source_target_pairs={{0,16},{1,17},{2,18},{3,19},{4,20},{5,21},{6,22},{7,23},{8,24},{9,... | collective-permute-start | bytes 208904 | tf_op jit(solution)/shard_map/ppermute | solution.py:599
  92.7 6.5 %collective-permute-start.19 = (f32[4,128,128]{2,1,0:T(8,128)S(1)}, f32[4,128,128]{2,1,0:T(8,128)S(1)}, u32[]{:S(2)}, u32[]{:S(2)}) collective-permute-start(f32[4,128,128]{2,1,0:T(8,128)S(1)} %get-tuple-element.70), channel_id=1, source_target_pairs={{0,2},{2,0},{4,6},{6,4},{8,10},{10,8},{12,14},{14,12},{16,18},{18,... | collective-permute-start | bytes 786440 | tf_op jit(solution)/shard_map/ppermute | solution.py:572
  92.7 9.8 %collective-permute-start.20 = (f32[4,128,128]{2,1,0:T(8,128)S(1)}, f32[4,128,128]{2,1,0:T(8,128)S(1)}, u32[]{:S(2)}, u32[]{:S(2)}) collective-permute-start(f32[4,128,128]{2,1,0:T(8,128)S(1)} %get-tuple-element.71), channel_id=1, source_target_pairs={{0,30},{2,4},{4,2},{6,8},{8,6},{10,12},{12,10},{14,16},{16,14},{18... | collective-permute-start | bytes 786440 | tf_op jit(solution)/shard_map/ppermute | solution.py:577
  102.6 3.2 %collective-permute-start.23 = (f32[136,128]{1,0:T(8,128)S(1)}, f32[136,128]{1,0:T(8,128)S(1)}, u32[]{:S(2)}, u32[]{:S(2)}) collective-permute-start(f32[136,128]{1,0:T(8,128)S(1)} %add_add_fusion.1), channel_id=1, source_target_pairs={{0,65},{1,0},{2,67},{3,2},{4,69},{5,4},{6,71},{7,6},{8,73},{9,8},{... | collective-permute-start | bytes 208904 | tf_op jit(solution)/shard_map/ppermute | solution.py:599
  102.6 4.4 %collective-permute-start.22 = (f32[136,128]{1,0:T(8,128)S(1)}, f32[136,128]{1,0:T(8,128)S(1)}, u32[]{:S(2)}, u32[]{:S(2)}) collective-permute-start(f32[136,128]{1,0:T(8,128)S(1)} %add_add_fusion.1), channel_id=1, source_target_pairs={{0,1},{1,64},{2,3},{3,66},{4,5},{5,68},{6,7},{7,70},{8,9},{9,72},{... | collective-permute-start | bytes 208904 | tf_op jit(solution)/shard_map/ppermute | solution.py:599
  104.0 4.7 %collective-permute-start.21 = (f32[136,128]{1,0:T(8,128)S(1)}, f32[136,128]{1,0:T(8,128)S(1)}, u32[]{:S(2)}, u32[]{:S(2)}) collective-permute-start(f32[136,128]{1,0:T(8,128)S(1)} %add_add_fusion.1), channel_id=1, source_target_pairs={{0,64},{1,65},{2,66},{3,67},{4,68},{5,69},{6,70},{7,71},{8,72},{9,... | collective-permute-start | bytes 208904 | tf_op jit(solution)/shard_map/ppermute | solution.py:599
  108.7 6.0 %collective-permute-start.24 = (f32[136,128]{1,0:T(8,128)S(1)}, f32[136,128]{1,0:T(8,128)S(1)}, u32[]{:S(2)}, u32[]{:S(2)}) collective-permute-start(f32[136,128]{1,0:T(8,128)S(1)} %add_add_fusion.keep), channel_id=1, source_target_pairs={{0,32},{32,0},{64,96},{96,64},{1,33},{33,1},{65,97},{97,65},{2,34}... | collective-permute-start | bytes 208904 | tf_op jit(solution)/shard_map/ppermute | solution.py:572
  (2 other events, 28.1 us)

commit v2 on v1

--- a/solution.py
+++ b/solution.py
@@ -13,7 +13,7 @@
 WIN = 128
 HALF = 64
 TALL = WIN + 8
-LEAD = 4
+LEAD = 5
 F32 = jnp.float32
 BF16 = jnp.bfloat16
 VMEM_LIMIT = 16 * 1024 * 1024
@@ -120,24 +120,38 @@
 
 
 def pack_kernel(pos, source, col1, col2, row1, row2, tile, sems):
-    fetch(source, tile, sems.at[0]).wait()
-    right = join(roll_half(tile[0, :, :, 128:]), tile[1, :, :, 128:])
-    left = join(tile[0, :, :, :128], roll_half(tile[1, :, :, :128]))
+    low = pos[2] * 64
+    loads = [
+        fetch(source.at[:, :, :, pl.ds(0, 128)], tile.at[0], sems.at[0]),
+        fetch(source.at[:, :, :, pl.ds(128, 128)], tile.at[1], sems.at[1]),
+        fetch(source.at[:, :, pl.ds(pl.multiple_of(64 - low, 64), 64), :], row1, sems.at[2]),
+        fetch(source.at[:, :, pl.ds(pl.multiple_of(low, 64), 64), :], row2, sems.at[3]),
+    ]
     even = pos[1] == 0
+    loads[0].wait()
+    left = join(tile[0, 0], roll_half(tile[0, 1]))
 
     @pl.when(even)
     def _():
+        col2[...] = left
+
+    @pl.when(jnp.logical_not(even))
+    def _():
+        col1[...] = left
+
+    loads[1].wait()
+    right = join(roll_half(tile[1, 0]), tile[1, 1])
+
+    @pl.when(even)
+    def _():
         col1[...] = right
-        col2[...] = left
 
     @pl.when(jnp.logical_not(even))
     def _():
-        col1[...] = left
         col2[...] = right
 
-    low = pos[2] * 64
-    row1[...] = tile[:, :, pl.ds(pl.multiple_of(64 - low, 64), 64), :]
-    row2[...] = tile[:, :, pl.ds(pl.multiple_of(low, 64), 64), :]
+    loads[2].wait()
+    loads[3].wait()
 
 
 def pack_corners_kernel(pos, col1, col2, first, second):
@@ -158,8 +172,8 @@
             out[:, :, 128:] = ring
 
 
-def inside(pos, value):
-    return jnp.where(pos[3] == 1, 0.0, value)
+def inside(pos, value, flag=3):
+    return jnp.where(pos[flag] == 1, 0.0, value)
 
 
 def load_window(ext, c, k, row, block, shift):
@@ -201,6 +215,7 @@
 
     cols[first] = inside(pos, cols[first])
     sides(slice(64, 192), cols[0], cols[1])
+    corners[1] = inside(pos, corners[1], 4)
     for i in range(2):
         sides(pl.ds(starts[i], 64), corners[i, :, :, :128], corners[i, :, :, 128:])
     for copy in far:
@@ -350,11 +365,8 @@
             fetch(measured_h.at[pl.ds(span[0], len(span))], measured, sems.at[slabs + 2]),
         ]
         held = start_ext(group, ext, held_h, sems, extra, slabs)
-        for copy in loads:
-            copy.wait()
+        loads[0].wait()
         right, left = step_pair(mats)
-        exit_right = (exits[0, 0], exits[0, 1])
-        exit_left = (exits[1, 0], exits[1, 1])
         fields = [pair(wave, i) for i in range(len(span))]
         for k in range(slabs):
             if k:
@@ -364,7 +376,11 @@
             if k < slabs - 1:
                 fields = apply_both(entering, right, left)
             else:
+                loads[1].wait()
+                exit_right = (exits[0, 0], exits[0, 1])
+                exit_left = (exits[1, 0], exits[1, 1])
                 fields = apply_both(entering, exit_right, exit_left)
+        loads[2].wait()
         total = jnp.zeros((8, 128), F32)
         far = []
         for i, p in enumerate(span):
@@ -406,11 +422,14 @@
         fetch(probe_h, probe, sems.at[slabs + 2]),
     ]
     held = start_ext(group, ext, held_h, sems, slabs + 3, slabs)
-    for copy in loads:
-        copy.wait()
+    loads[0].wait()
     right, left = step_pair(mats)
 
     def incident(k, i):
+        if i == 0 and k == slabs - 1:
+            loads[1].wait()
+        if i == 0 and k == 0:
+            loads[2].wait()
         return (probe[0], probe[1]) if k == 0 else pair(psi.at[k - 1], i)
 
     grads = ("inner", [pair(grad, i) for i in range(len(span))])
@@ -572,9 +591,20 @@
     return lax.ppermute(value, axis, pairs)
 
 
-def swap_odd_ring(value, axis):
-    size = lax.axis_size(axis)
-    return lax.ppermute(value, axis, [(i, (((i - 1) % size) ^ 1) + 1 if i not in (0, size - 1) else size - 1 - i) for i in range(size)])
+def closed(value, sizes, move):
+    rows, cols = sizes[:2]
+    pairs = [(a * cols + b, move(a, b)[0] * cols + move(a, b)[1]) for a in range(rows) for b in range(cols)]
+    return lax.ppermute(value, ("sx", "sy"), pairs)
+
+
+def swap_odd_columns(value, sizes):
+    last = sizes[1] - 1
+    return closed(value, sizes, lambda a, b: (a ^ 1, b) if b in (0, last) else (a, ((b - 1) ^ 1) + 1))
+
+
+def swap_odd_rows(value, sizes):
+    last = sizes[0] - 1
+    return closed(value, sizes, lambda a, b: (a, b ^ 1) if a in (0, last) else (((a - 1) ^ 1) + 1, b))
 
 
 def swap_odd(value, axis):
@@ -621,7 +651,10 @@
     core = lax.axis_index("sx") % 2
     column = lax.axis_index("sy")
     edge_column = (column == 0) | (column == lax.axis_size("sy") - 1)
-    where = jnp.stack([lax.axis_index("depth"), column % 2, core, edge_column.astype(jnp.int32)]).astype(jnp.int32)
+    edge_row = (lax.axis_index("sx") == 0) | (lax.axis_index("sx") == lax.axis_size("sx") - 1)
+    where = jnp.stack(
+        [lax.axis_index("depth"), column % 2, core, edge_column.astype(jnp.int32), edge_row.astype(jnp.int32)]
+    ).astype(jnp.int32)
     pos = jnp.concatenate([where, scan_offsets.reshape(-1), pattern_shifts.reshape(-1)])
     sizes = (lax.axis_size("sx"), lax.axis_size("sy"), lax.axis_size("depth"))
 
@@ -645,12 +678,12 @@
     probe = vmem(probe_wave.shape)
 
     col1, col2, row1, row2 = call(
-        pack_kernel, [strip, strip, side, side], [where], [transmission], [vmem(tile), sems(1)], hbm=(0,), fixed=(0,)
-    )
-    col1, col2 = swap(col1, "sy"), swap_odd_ring(col2, "sy")
+        pack_kernel, [strip, strip, side, side], [where], [transmission], [vmem((2, 2) + strip), sems(4)], hbm=(0,), fixed=(0,)
+    )
+    col1, col2 = swap(col1, "sy"), swap_odd_columns(col2, sizes)
     row1, row2 = swap(row1, "sx"), swap_odd(row2, "sx")
     crn1, crn2 = call(pack_corners_kernel, [corner, corner], [where], [col1, col2])
-    crn1, crn2 = swap(crn1, "sx"), swap_odd(crn2, "sx")
+    crn1, crn2 = swap(crn1, "sx"), swap_odd_rows(crn2, sizes)
     spans = (tuple(range(count // 2)), tuple(range(count // 2, count)))
     assembly = [vmem(ext)]
     parts = [vmem((2,) + strip), vmem((2,) + corner)]
@@ -665,7 +698,7 @@
         hbm_out=(2,),
         fixed=(0, 1, 8),
     )
-    wave_a = lax.ppermute(wave_a, "depth", [(0, 1)])
+    wave_a = lax.ppermute(wave_a, "depth", [(0, 1), (1, 0)])
     wave_b, psi_b = call(
         functools.partial(forward_second_kernel, spans),
         [field, inner],
@@ -713,7 +746,7 @@
         fixed=(2, 3, 4),
         aliases={6: 2},
     )
-    grad_b = lax.ppermute(grad_b, "depth", [(1, 0)])
+    grad_b = lax.ppermute(grad_b, "depth", [(1, 0), (0, 1)])
     total, edge = call(
         functools.partial(backward_first_kernel, spans[0]),
         [(2, WIN, WIN), ext],
@@ -747,11 +780,11 @@
         [vmem((2, 2) + strip), sems(2)], hbm=(0,),
     )
     part, col1, col2 = lax.optimization_barrier((part, col1, col2))
-    col1, col2 = swap(col1, "sy"), swap_odd_ring(col2, "sy")
-    part = ring_sum(part, sizes, turn_z)
+    col1, col2 = swap(col1, "sy"), swap_odd_columns(col2, sizes)
+    part = ring_sum(part, sizes, turn_y)
     part, col1, col2 = lax.optimization_barrier((part, col1, col2))
     (out,) = call(fold_kernel, [tile], [where], [edge, row1, row2, col1, col2], [sems(1)], hbm=(0,))
-    part = ring_sum(part, sizes, turn_y)
+    part = ring_sum(part, sizes, turn_z)
     other = swap(part, "sx")
     positions = count * sizes[0] * sizes[1]
     scales = jnp.array([1.0 / positions, 1.0 / (positions * WIN * WIN)], F32)

time: 117 us -> 111 us (0.949)
  waiting for transfers between devices: 36.6 us -> 21.1 us
  starting transfers between devices: 45.6 us -> 56 us
    ppermute x1, waiting for transfers between devices: 10.2 us -> 0.01 us  [local(): grad_a = lax.ppermute(grad_a, 'depth', [(1, 0)])]
    ppermute x4 -> x5, starting transfers between devices: 11 us -> 19.4 us  [the longest x1 13.7 us: local(): grad_b = lax.ppermute(grad_b, 'depth', [(1, 0), (0, 1)])]
    ppermute x9, starting transfers between devices: 7.72 us -> 15.8 us  [ring_sum(): got.append(lax.ppermute(value, AXES, pairs))]
    ppermute x3 -> x2, starting transfers between devices: 15.5 us -> 8.45 us  [swap_odd(): lax.ppermute(value, axis, [(i, (i - 1 ^ 1) + 1) for i in range(1, size -...]
    ppermute x3 -> x2, waiting for transfers between devices: 4.76 us -> 0.01 us  [swap_odd(): lax.ppermute(value, axis, [(i, (i - 1 ^ 1) + 1) for i in range(1, size -...]
    ppermute x4 -> x5, waiting for transfers between devices: 7 us -> 4.98 us  [the longest x3 2.46 us: closed(): return lax.ppermute(value, ('sx', 'sy'), pairs)]
  transfers between devices with their start and end apart: 25 -> 25, of which waited for: 15 -> 10; matrix products, arithmetic and copies ran while one was open for 2% -> 2% of each run, Pallas kernels for 13% -> 14%
where the time goes in v2:
time: 111 us
  starting transfers between devices  56 us (50%)
  Pallas kernels  30.7 us (28%)
  waiting for transfers between devices  21.1 us (19%)
  local copies, waits for them, and re-layouts  1.88 us (2%)
    pallas_call x12, Pallas kernels, call(): pl.pallas_call(kernel, out_shape=outs, in_specs=[pl.BlockSpec(memory_spac...  30.7 us
    ppermute x9, starting transfers between devices, ring_sum(): got.append(lax.ppermute(value, AXES, pairs))  15.8 us
    ppermute x1, starting transfers between devices, local(): grad_b = lax.ppermute(grad_b, 'depth', [(1, 0), (0, 1)])  13.7 us
    ppermute x9, waiting for transfers between devices, ring_sum(): got.append(lax.ppermute(value, AXES, pairs))  10.8 us
    ppermute x7, starting transfers between devices, swap(): return lax.ppermute(value, axis, pairs)  9.55 us
    ppermute x2, starting transfers between devices, swap_odd(): lax.ppermute(value, axis, [(i, (i - 1 ^ 1) + 1) for i in range(1, size -...  8.45 us
    ppermute x3, starting transfers between devices, closed(): return lax.ppermute(value, ('sx', 'sy'), pairs)  5.64 us
    ppermute x7, waiting for transfers between devices, swap(): return lax.ppermute(value, axis, pairs)  4.04 us
  transfers between devices with their start and end apart: 25, of which 10 were waited for; matrix products, arithmetic and copies ran while one was open for 2% of the time, Pallas kernels for 14%

profile of v2, /device:TPU:1, one launch (start us, length us, event | category | flops | bytes accessed | tf_op | source)
XLA Modules:
  0.0 110.8 jit_solution(9267240649018190979)
XLA Ops:
  0.7 2.1 %shard_map.103 = (f32[4,128,128]{2,1,0:T(8,128)S(1)}, f32[4,128,128]{2,1,0:T(8,128)S(1)}, f32[2,4,64,256]{3,2,1,0:T(8,128)S(1)}, f32[2,4,64,256]{3,2,1,0:T(8,128)S(1)}) custom-call(s32[5]{0:T(128)S(1)} %stack.31.pos, f32[2,4,128,256]{3,2,1,0:T(8,128)} %tile.3), custom_call_target="tpu_custom_call" | custom-call | bytes 2621440 | tf_op jit(solution)/shard_map/pallas_call | solution.py:573
  2.9 2.1 %collective-permute-start = (f32[4,128,128]{2,1,0:T(8,128)S(1)}, f32[4,128,128]{2,1,0:T(8,128)S(1)}, u32[]{:S(2)}, u32[]{:S(2)}) collective-permute-start(f32[4,128,128]{2,1,0:T(8,128)S(1)} %get-tuple-element.40), channel_id=1, source_target_pairs={{0,2},{2,0},{4,6},{6,4},{8,10},{10,8},{12,14},{14,12},{16,18},{18,... | collective-permute-start | bytes 786440 | tf_op jit(solution)/shard_map/ppermute | solution.py:591
  5.9 5.2 %collective-permute-start.3 = (f32[2,4,64,256]{3,2,1,0:T(8,128)S(1)}, f32[2,4,64,256]{3,2,1,0:T(8,128)S(1)}, u32[]{:S(2)}, u32[]{:S(2)}) collective-permute-start(f32[2,4,64,256]{3,2,1,0:T(8,128)S(1)} %get-tuple-element.43), channel_id=1, source_target_pairs={{32,64},{64,32},{33,65},{65,33},{34,66},{66,34},{35,67},{67,35},{3... | collective-permute-start | bytes 1572872 | tf_op jit(solution)/shard_map/ppermute | solution.py:612
  13.5 3.1 %collective-permute-start.5 = (f32[4,64,256]{2,1,0:T(8,128)S(1)}, f32[4,64,256]{2,1,0:T(8,128)S(1)}, u32[]{:S(2)}, u32[]{:S(2)}) collective-permute-start(f32[4,64,256]{2,1,0:T(8,128)S(1)} %get-tuple-element.45), channel_id=1, source_target_pairs={{0,2},{2,0},{4,6},{6,4},{8,10},{10,8},{12,14},{14,12},{16,18},{18,... | collective-permute-start | bytes 786440 | tf_op jit(solution)/shard_map/ppermute | solution.py:597
  18.4 2.5 %collective-permute-done.5.crn2_h = f32[4,64,256]{2,1,0:T(8,128)S(1)} collective-permute-done((f32[4,64,256]{2,1,0:T(8,128)S(1)}, f32[4,64,256]{2,1,0:T(8,128)S(1)}, u32[]{:S(2)}, u32[]{:S(2)}) %collective-permute-start.5) | collective-permute-done | bytes 262176 | tf_op jit(solution)/shard_map/ppermute | solution.py:597
  20.8 5.1 %shard_map.105 = (f32[2,2,128,128]{3,2,1,0:T(8,128)S(1)}, f32[4,4,2,128,128]{4,3,2,1,0:T(8,128)S(1)}, f32[3,2,2,128,128]{4,3,2,1,0:T(8,128)S(1)}) custom-call(s32[21]{0:T(128)S(1)} %concatenate.4.pos, f32[2,128,128]{2,1,0:T(8,128)} %probe_h.7, f32[2,4,128,256]{3,2,1,0:T(8,128)} %tile.3, f32[4,128,128]{2,1,0:T(8,128)S(1)} %collective-permute-done.col1.col1_h, ...), custom_call_target="tpu_custom_call" | custom-call | flops 805306368 | bytes 6946816 | tf_op jit(solution)/shard_map/pallas_call | solution.py:573
  26.0 4.5 %shard_map.106 = (f32[2,2,128,128]{3,2,1,0:T(8,128)S(1)}, f32[3,2,2,128,128]{4,3,2,1,0:T(8,128)S(1)}) custom-call(s32[21]{0:T(128)S(1)} %concatenate.4.pos, f32[2,128,128]{2,1,0:T(8,128)} %probe_h.7, f32[4,4,2,128,128]{4,3,2,1,0:T(8,128)S(1)} %get-tuple-element.46.win, bf16[2,256,256]{2,1,0:T(8,128)(2,1)} %constant.42.clone.mats_h), custom_call_target="tpu_custom_call" | custom-call | flops 805306368 | bytes 3801088 | tf_op jit(solution)/shard_map/pallas_call | solution.py:573
  32.5 1.7 %collective-permute-done.7.wave = f32[2,2,128,128]{3,2,1,0:T(8,128)S(1)} collective-permute-done((f32[2,2,128,128]{3,2,1,0:T(8,128)S(1)}, f32[2,2,128,128]{3,2,1,0:T(8,128)S(1)}, u32[]{:S(2)}, u32[]{:S(2)}) %collective-permute-start.7) | collective-permute-done | bytes 262176 | tf_op jit(solution)/shard_map/ppermute | solution.py:701
  34.8 1.5 %collective-permute-start.9 = (f32[2,2,128,128]{3,2,1,0:T(8,128)S(1)}, f32[2,2,128,128]{3,2,1,0:T(8,128)S(1)}, u32[]{:S(2)}, u32[]{:S(2)}) collective-permute-start(f32[2,2,128,128]{3,2,1,0:T(8,128)S(1)} %get-tuple-element.53), channel_id=1, source_target_pairs={{1,0},{3,2},{5,4},{7,6},{9,8},{11,10},{13,12},{15,14},{17,16},{19,... | collective-permute-start | bytes 786440 | tf_op jit(solution)/shard_map/ppermute | solution.py:736
  38.2 13.7 %collective-permute-start.8 = (f32[2,2,128,128]{3,2,1,0:T(8,128)S(1)}, f32[2,2,128,128]{3,2,1,0:T(8,128)S(1)}, u32[]{:S(2)}, u32[]{:S(2)}) collective-permute-start(f32[2,2,128,128]{3,2,1,0:T(8,128)S(1)} %get-tuple-element.51), channel_id=1, source_target_pairs={{1,0},{0,1},{3,2},{2,3},{5,4},{4,5},{7,6},{6,7},{9,8},{8,9},{11,10... | collective-permute-start | bytes 786440 | tf_op jit(solution)/shard_map/ppermute | solution.py:749
  51.9 5.5 %shard_map.110 = (f32[2,128,128]{2,1,0:T(8,128)S(1)}, f32[2,4,264,512]{3,2,1,0:T(8,128)S(1)}) custom-call(s32[21]{0:T(128)S(1)} %concatenate.4.pos, f32[2,2,128,128]{3,2,1,0:T(8,128)S(1)} %collective-permute-done.9.grad, f32[4,4,2,128,128]{4,3,2,1,0:T(8,128)S(1)} %get-tuple-element.46.win, ...), custom_call_target="tpu_custom_call", output_to_operand_aliasing={{1}: (6, {})} | custom-call | flops 805306368 | bytes 12582912 | tf_op jit(solution)/shard_map/pallas_call | solution.py:573
  58.3 6.0 %shard_map.111 = (f32[136,128]{1,0:T(8,128)S(1)}, f32[136,128]{1,0:T(8,128)S(1)}, f32[2,4,264,512]{3,2,1,0:T(8,128)S(1)}, f32[4,64,768]{2,1,0:T(8,128)S(1)}, f32[4,64,768]{2,1,0:T(8,128)S(1)}) custom-call(s32[21]{0:T(128)S(1)} %concatenate.4.pos, f32[2,2,128,128]{3,2,1,0:T(8,128)S(1)} %collective-permute-done.8.grad, ...), custom_call_target="tpu_custom_call", output_to_operand_aliasing={{2}: (6, {})} | custom-call | flops 805306368 | bytes 14299136 | tf_op jit(solution)/shard_map/pallas_call | solution.py:573
  65.3 3.2 %collective-permute-start.15 = (f32[4,64,768]{2,1,0:T(8,128)S(1)}, f32[4,64,768]{2,1,0:T(8,128)S(1)}, u32[]{:S(2)}, u32[]{:S(2)}) collective-permute-start(f32[4,64,768]{2,1,0:T(8,128)S(1)} %get-tuple-element.63), channel_id=1, source_target_pairs={{32,64},{64,32},{33,65},{65,33},{34,66},{66,34},{35,67},{67,35},{3... | collective-permute-start | bytes 2359304 | tf_op jit(solution)/shard_map/ppermute | solution.py:612
  69.9 5.0 %collective-permute-start.13 = (f32[136,128]{1,0:T(8,128)S(1)}, f32[136,128]{1,0:T(8,128)S(1)}, u32[]{:S(2)}, u32[]{:S(2)}) collective-permute-start(f32[136,128]{1,0:T(8,128)S(1)} %add.39), channel_id=1, source_target_pairs={{0,6},{1,7},{2,0},{3,1},{4,2},{5,3},{6,4},{7,5},{8,14},{9,15},{10,... | collective-permute-start | bytes 208904 | tf_op jit(solution)/shard_map/ppermute | solution.py:629
  76.2 5.1 %collective-permute-done.12 = f32[136,128]{1,0:T(8,128)S(1)} collective-permute-done((f32[136,128]{1,0:T(8,128)S(1)}, f32[136,128]{1,0:T(8,128)S(1)}, u32[]{:S(2)}, u32[]{:S(2)}) %collective-permute-start.12) | collective-permute-done | bytes 69664 | tf_op jit(solution)/shard_map/ppermute | solution.py:629
  82.5 1.5 %collective-permute-start.17 = (f32[136,128]{1,0:T(8,128)S(1)}, f32[136,128]{1,0:T(8,128)S(1)}, u32[]{:S(2)}, u32[]{:S(2)}) collective-permute-start(f32[136,128]{1,0:T(8,128)S(1)} %add_add_fusion.2), channel_id=1, source_target_pairs={{0,1},{1,64},{2,3},{3,66},{4,5},{5,68},{6,7},{7,70},{8,9},{9,72},{... | collective-permute-start | bytes 208904 | tf_op jit(solution)/shard_map/ppermute | solution.py:629
  84.0 1.7 %collective-permute-start.16 = (f32[136,128]{1,0:T(8,128)S(1)}, f32[136,128]{1,0:T(8,128)S(1)}, u32[]{:S(2)}, u32[]{:S(2)}) collective-permute-start(f32[136,128]{1,0:T(8,128)S(1)} %add_add_fusion.2), channel_id=1, source_target_pairs={{0,64},{1,65},{2,66},{3,67},{4,68},{5,69},{6,70},{7,71},{8,72},{9,... | collective-permute-start | bytes 208904 | tf_op jit(solution)/shard_map/ppermute | solution.py:629
  85.7 1.6 %collective-permute-start.20 = (f32[4,128,128]{2,1,0:T(8,128)S(1)}, f32[4,128,128]{2,1,0:T(8,128)S(1)}, u32[]{:S(2)}, u32[]{:S(2)}) collective-permute-start(f32[4,128,128]{2,1,0:T(8,128)S(1)} %get-tuple-element.71), channel_id=1, source_target_pairs={{0,32},{2,4},{4,2},{6,8},{8,6},{10,12},{12,10},{14,16},{16,14},{18... | collective-permute-start | bytes 786440 | tf_op jit(solution)/shard_map/ppermute | solution.py:597
  87.3 1.8 %collective-permute-done.16 = f32[136,128]{1,0:T(8,128)S(1)} collective-permute-done((f32[136,128]{1,0:T(8,128)S(1)}, f32[136,128]{1,0:T(8,128)S(1)}, u32[]{:S(2)}, u32[]{:S(2)}) %collective-permute-start.16) | collective-permute-done | bytes 69664 | tf_op jit(solution)/shard_map/ppermute | solution.py:629
  89.1 2.8 %collective-permute-done.19.col1 = f32[4,128,128]{2,1,0:T(8,128)S(1)} collective-permute-done((f32[4,128,128]{2,1,0:T(8,128)S(1)}, f32[4,128,128]{2,1,0:T(8,128)S(1)}, u32[]{:S(2)}, u32[]{:S(2)}) %collective-permute-start.19) | collective-permute-done | bytes 262176 | tf_op jit(solution)/shard_map/ppermute | solution.py:591
  91.9 4.9 %collective-permute-start.23 = (f32[136,128]{1,0:T(8,128)S(1)}, f32[136,128]{1,0:T(8,128)S(1)}, u32[]{:S(2)}, u32[]{:S(2)}) collective-permute-start(f32[136,128]{1,0:T(8,128)S(1)} %add_add_fusion.1), channel_id=1, source_target_pairs={{0,24},{1,25},{2,26},{3,27},{4,28},{5,29},{6,30},{7,31},{8,0},{9,1... | collective-permute-start | bytes 208904 | tf_op jit(solution)/shard_map/ppermute | solution.py:629
  98.2 3.7 %collective-permute-done.22 = f32[136,128]{1,0:T(8,128)S(1)} collective-permute-done((f32[136,128]{1,0:T(8,128)S(1)}, f32[136,128]{1,0:T(8,128)S(1)}, u32[]{:S(2)}, u32[]{:S(2)}) %collective-permute-start.22) | collective-permute-done | bytes 69664 | tf_op jit(solution)/shard_map/ppermute | solution.py:629
  102.0 5.3 %collective-permute-start.24 = (f32[136,128]{1,0:T(8,128)S(1)}, f32[136,128]{1,0:T(8,128)S(1)}, u32[]{:S(2)}, u32[]{:S(2)}) collective-permute-start(f32[136,128]{1,0:T(8,128)S(1)} %add_add_fusion.keep), channel_id=1, source_target_pairs={{0,32},{32,0},{64,96},{96,64},{1,33},{33,1},{65,97},{97,65},{2,34}... | collective-permute-start | bytes 208904 | tf_op jit(solution)/shard_map/ppermute | solution.py:591
  107.3 2.0 %shard_map.113 = f32[2,4,128,256]{3,2,1,0:T(8,128)} custom-call(s32[5]{0:T(128)S(1)} %stack.31.pos, f32[2,4,264,512]{3,2,1,0:T(8,128)S(1)} %get-tuple-element.59.ext_h, f32[4,64,768]{2,1,0:T(8,128)S(1)} %collective-permute-done.14.row1, f32[4,64,768]{2,1,0:T(8,128)S(1)} %collective-permute-done.15.row2, f32[4,128,128]{2,1,0:T(8,128)S(1)} %collective-permute-done.19.col1, ...), custom_call_target="tpu_custom_call" | custom-call | bytes 7471104 | tf_op jit(solution)/shard_map/pallas_call | solution.py:573
  (50 shorter events, 18.1 us)
Async XLA Ops:
  2.9 8.3 %collective-permute-start = (f32[4,128,128]{2,1,0:T(8,128)S(1)}, f32[4,128,128]{2,1,0:T(8,128)S(1)}, u32[]{:S(2)}, u32[]{:S(2)}) collective-permute-start(f32[4,128,128]{2,1,0:T(8,128)S(1)} %get-tuple-element.40), channel_id=1, source_target_pairs={{0,2},{2,0},{4,6},{6,4},{8,10},{10,8},{12,14},{14,12},{16,18},{18,... | collective-permute-start | bytes 786440 | tf_op jit(solution)/shard_map/ppermute | solution.py:591
  5.0 6.2 %collective-permute-start.1 = (f32[4,128,128]{2,1,0:T(8,128)S(1)}, f32[4,128,128]{2,1,0:T(8,128)S(1)}, u32[]{:S(2)}, u32[]{:S(2)}) collective-permute-start(f32[4,128,128]{2,1,0:T(8,128)S(1)} %get-tuple-element.41), channel_id=1, source_target_pairs={{0,32},{2,4},{4,2},{6,8},{8,6},{10,12},{12,10},{14,16},{16,14},{18... | collective-permute-start | bytes 786440 | tf_op jit(solution)/shard_map/ppermute | solution.py:597
  5.9 14.9 %collective-permute-start.2 = (f32[2,4,64,256]{3,2,1,0:T(8,128)S(1)}, f32[2,4,64,256]{3,2,1,0:T(8,128)S(1)}, u32[]{:S(2)}, u32[]{:S(2)}) collective-permute-start(f32[2,4,64,256]{3,2,1,0:T(8,128)S(1)} %get-tuple-element.42), channel_id=1, source_target_pairs={{0,32},{32,0},{64,96},{96,64},{1,33},{33,1},{65,97},{97,65},{2,34}... | collective-permute-start | bytes 1572872 | tf_op jit(solution)/shard_map/ppermute | solution.py:591
  5.9 14.9 %collective-permute-start.3 = (f32[2,4,64,256]{3,2,1,0:T(8,128)S(1)}, f32[2,4,64,256]{3,2,1,0:T(8,128)S(1)}, u32[]{:S(2)}, u32[]{:S(2)}) collective-permute-start(f32[2,4,64,256]{3,2,1,0:T(8,128)S(1)} %get-tuple-element.43), channel_id=1, source_target_pairs={{32,64},{64,32},{33,65},{65,33},{34,66},{66,34},{35,67},{67,35},{3... | collective-permute-start | bytes 1572872 | tf_op jit(solution)/shard_map/ppermute | solution.py:612
  12.5 5.9 %collective-permute-start.4 = (f32[4,64,256]{2,1,0:T(8,128)}, f32[4,64,256]{2,1,0:T(8,128)S(1)}, u32[]{:S(2)}, u32[]{:S(2)}) collective-permute-start(f32[4,64,256]{2,1,0:T(8,128)} %get-tuple-element.44), channel_id=1, source_target_pairs={{0,32},{32,0},{64,96},{96,64},{1,33},{33,1},{65,97},{97,65},{2,34}... | collective-permute-start | bytes 786440 | tf_op jit(solution)/shard_map/ppermute | solution.py:591
  13.5 7.3 %collective-permute-start.5 = (f32[4,64,256]{2,1,0:T(8,128)S(1)}, f32[4,64,256]{2,1,0:T(8,128)S(1)}, u32[]{:S(2)}, u32[]{:S(2)}) collective-permute-start(f32[4,64,256]{2,1,0:T(8,128)S(1)} %get-tuple-element.45), channel_id=1, source_target_pairs={{0,2},{2,0},{4,6},{6,4},{8,10},{10,8},{12,14},{14,12},{16,18},{18,... | collective-permute-start | bytes 786440 | tf_op jit(solution)/shard_map/ppermute | solution.py:597
  25.9 8.2 %collective-permute-start.7 = (f32[2,2,128,128]{3,2,1,0:T(8,128)S(1)}, f32[2,2,128,128]{3,2,1,0:T(8,128)S(1)}, u32[]{:S(2)}, u32[]{:S(2)}) collective-permute-start(f32[2,2,128,128]{3,2,1,0:T(8,128)S(1)} %get-tuple-element.48), channel_id=1, source_target_pairs={{0,1},{1,0},{2,3},{3,2},{4,5},{5,4},{6,7},{7,6},{8,9},{9,8},{10,11... | collective-permute-start | bytes 786440 | tf_op jit(solution)/shard_map/ppermute | solution.py:701
  30.5 7.0 %collective-permute-start.6 = (f32[2,2,128,128]{3,2,1,0:T(8,128)S(1)}, f32[2,2,128,128]{3,2,1,0:T(8,128)S(1)}, u32[]{:S(2)}, u32[]{:S(2)}) collective-permute-start(f32[2,2,128,128]{3,2,1,0:T(8,128)S(1)} %get-tuple-element.47), channel_id=1, source_target_pairs={{0,1},{2,3},{4,5},{6,7},{8,9},{10,11},{12,13},{14,15},{16,17},{18,... | collective-permute-start | bytes 786440 | tf_op jit(solution)/shard_map/ppermute | solution.py:713
  34.8 17.1 %collective-permute-start.9 = (f32[2,2,128,128]{3,2,1,0:T(8,128)S(1)}, f32[2,2,128,128]{3,2,1,0:T(8,128)S(1)}, u32[]{:S(2)}, u32[]{:S(2)}) collective-permute-start(f32[2,2,128,128]{3,2,1,0:T(8,128)S(1)} %get-tuple-element.53), channel_id=1, source_target_pairs={{1,0},{3,2},{5,4},{7,6},{9,8},{11,10},{13,12},{15,14},{17,16},{19,... | collective-permute-start | bytes 786440 | tf_op jit(solution)/shard_map/ppermute | solution.py:736
  38.2 20.1 %collective-permute-start.8 = (f32[2,2,128,128]{3,2,1,0:T(8,128)S(1)}, f32[2,2,128,128]{3,2,1,0:T(8,128)S(1)}, u32[]{:S(2)}, u32[]{:S(2)}) collective-permute-start(f32[2,2,128,128]{3,2,1,0:T(8,128)S(1)} %get-tuple-element.51), channel_id=1, source_target_pairs={{1,0},{0,1},{3,2},{2,3},{5,4},{4,5},{7,6},{6,7},{9,8},{8,9},{11,10... | collective-permute-start | bytes 786440 | tf_op jit(solution)/shard_map/ppermute | solution.py:749
  64.3 17.1 %collective-permute-start.14 = (f32[4,64,768]{2,1,0:T(8,128)S(1)}, f32[4,64,768]{2,1,0:T(8,128)S(1)}, u32[]{:S(2)}, u32[]{:S(2)}) collective-permute-start(f32[4,64,768]{2,1,0:T(8,128)S(1)} %get-tuple-element.62), channel_id=1, source_target_pairs={{0,32},{32,0},{64,96},{96,64},{1,33},{33,1},{65,97},{97,65},{2,34}... | collective-permute-start | bytes 2359304 | tf_op jit(solution)/shard_map/ppermute | solution.py:591
  65.3 16.2 %collective-permute-start.15 = (f32[4,64,768]{2,1,0:T(8,128)S(1)}, f32[4,64,768]{2,1,0:T(8,128)S(1)}, u32[]{:S(2)}, u32[]{:S(2)}) collective-permute-start(f32[4,64,768]{2,1,0:T(8,128)S(1)} %get-tuple-element.63), channel_id=1, source_target_pairs={{32,64},{64,32},{33,65},{65,33},{34,66},{66,34},{35,67},{67,35},{3... | collective-permute-start | bytes 2359304 | tf_op jit(solution)/shard_map/ppermute | solution.py:612
  69.9 6.4 %collective-permute-start.13 = (f32[136,128]{1,0:T(8,128)S(1)}, f32[136,128]{1,0:T(8,128)S(1)}, u32[]{:S(2)}, u32[]{:S(2)}) collective-permute-start(f32[136,128]{1,0:T(8,128)S(1)} %add.39), channel_id=1, source_target_pairs={{0,6},{1,7},{2,0},{3,1},{4,2},{5,3},{6,4},{7,5},{8,14},{9,15},{10,... | collective-permute-start | bytes 208904 | tf_op jit(solution)/shard_map/ppermute | solution.py:629
  74.9 6.5 %collective-permute-start.12 = (f32[136,128]{1,0:T(8,128)S(1)}, f32[136,128]{1,0:T(8,128)S(1)}, u32[]{:S(2)}, u32[]{:S(2)}) collective-permute-start(f32[136,128]{1,0:T(8,128)S(1)} %add.39), channel_id=1, source_target_pairs={{0,2},{1,3},{2,4},{3,5},{4,6},{5,7},{6,0},{7,1},{8,10},{9,11},{10,... | collective-permute-start | bytes 208904 | tf_op jit(solution)/shard_map/ppermute | solution.py:629
  74.9 6.5 %collective-permute-start.11 = (f32[136,128]{1,0:T(8,128)S(1)}, f32[136,128]{1,0:T(8,128)S(1)}, u32[]{:S(2)}, u32[]{:S(2)}) collective-permute-start(f32[136,128]{1,0:T(8,128)S(1)} %add.39), channel_id=1, source_target_pairs={{0,4},{1,5},{2,6},{3,7},{4,0},{5,1},{6,2},{7,3},{8,12},{9,13},{10,... | collective-permute-start | bytes 208904 | tf_op jit(solution)/shard_map/ppermute | solution.py:629
  82.4 4.9 %collective-permute-start.18 = (f32[136,128]{1,0:T(8,128)S(1)}, f32[136,128]{1,0:T(8,128)S(1)}, u32[]{:S(2)}, u32[]{:S(2)}) collective-permute-start(f32[136,128]{1,0:T(8,128)S(1)} %add_add_fusion.2), channel_id=1, source_target_pairs={{0,65},{1,0},{2,67},{3,2},{4,69},{5,4},{6,71},{7,6},{8,73},{9,8},{... | collective-permute-start | bytes 208904 | tf_op jit(solution)/shard_map/ppermute | solution.py:629
  82.5 4.8 %collective-permute-start.17 = (f32[136,128]{1,0:T(8,128)S(1)}, f32[136,128]{1,0:T(8,128)S(1)}, u32[]{:S(2)}, u32[]{:S(2)}) collective-permute-start(f32[136,128]{1,0:T(8,128)S(1)} %add_add_fusion.2), channel_id=1, source_target_pairs={{0,1},{1,64},{2,3},{3,66},{4,5},{5,68},{6,7},{7,70},{8,9},{9,72},{... | collective-permute-start | bytes 208904 | tf_op jit(solution)/shard_map/ppermute | solution.py:629
  84.0 5.1 %collective-permute-start.16 = (f32[136,128]{1,0:T(8,128)S(1)}, f32[136,128]{1,0:T(8,128)S(1)}, u32[]{:S(2)}, u32[]{:S(2)}) collective-permute-start(f32[136,128]{1,0:T(8,128)S(1)} %add_add_fusion.2), channel_id=1, source_target_pairs={{0,64},{1,65},{2,66},{3,67},{4,68},{5,69},{6,70},{7,71},{8,72},{9,... | collective-permute-start | bytes 208904 | tf_op jit(solution)/shard_map/ppermute | solution.py:629
  85.7 6.2 %collective-permute-start.19 = (f32[4,128,128]{2,1,0:T(8,128)S(1)}, f32[4,128,128]{2,1,0:T(8,128)S(1)}, u32[]{:S(2)}, u32[]{:S(2)}) collective-permute-start(f32[4,128,128]{2,1,0:T(8,128)S(1)} %get-tuple-element.70), channel_id=1, source_target_pairs={{0,2},{2,0},{4,6},{6,4},{8,10},{10,8},{12,14},{14,12},{16,18},{18,... | collective-permute-start | bytes 786440 | tf_op jit(solution)/shard_map/ppermute | solution.py:591
  85.7 6.2 %collective-permute-start.20 = (f32[4,128,128]{2,1,0:T(8,128)S(1)}, f32[4,128,128]{2,1,0:T(8,128)S(1)}, u32[]{:S(2)}, u32[]{:S(2)}) collective-permute-start(f32[4,128,128]{2,1,0:T(8,128)S(1)} %get-tuple-element.71), channel_id=1, source_target_pairs={{0,32},{2,4},{4,2},{6,8},{8,6},{10,12},{12,10},{14,16},{16,14},{18... | collective-permute-start | bytes 786440 | tf_op jit(solution)/shard_map/ppermute | solution.py:597
  91.9 6.3 %collective-permute-start.23 = (f32[136,128]{1,0:T(8,128)S(1)}, f32[136,128]{1,0:T(8,128)S(1)}, u32[]{:S(2)}, u32[]{:S(2)}) collective-permute-start(f32[136,128]{1,0:T(8,128)S(1)} %add_add_fusion.1), channel_id=1, source_target_pairs={{0,24},{1,25},{2,26},{3,27},{4,28},{5,29},{6,30},{7,31},{8,0},{9,1... | collective-permute-start | bytes 208904 | tf_op jit(solution)/shard_map/ppermute | solution.py:629
  96.8 5.1 %collective-permute-start.22 = (f32[136,128]{1,0:T(8,128)S(1)}, f32[136,128]{1,0:T(8,128)S(1)}, u32[]{:S(2)}, u32[]{:S(2)}) collective-permute-start(f32[136,128]{1,0:T(8,128)S(1)} %add_add_fusion.1), channel_id=1, source_target_pairs={{0,8},{1,9},{2,10},{3,11},{4,12},{5,13},{6,14},{7,15},{8,16},{9,17... | collective-permute-start | bytes 208904 | tf_op jit(solution)/shard_map/ppermute | solution.py:629
  96.9 5.1 %collective-permute-start.21 = (f32[136,128]{1,0:T(8,128)S(1)}, f32[136,128]{1,0:T(8,128)S(1)}, u32[]{:S(2)}, u32[]{:S(2)}) collective-permute-start(f32[136,128]{1,0:T(8,128)S(1)} %add_add_fusion.1), channel_id=1, source_target_pairs={{0,16},{1,17},{2,18},{3,19},{4,20},{5,21},{6,22},{7,23},{8,24},{9,... | collective-permute-start | bytes 208904 | tf_op jit(solution)/shard_map/ppermute | solution.py:629
  102.0 7.3 %collective-permute-start.24 = (f32[136,128]{1,0:T(8,128)S(1)}, f32[136,128]{1,0:T(8,128)S(1)}, u32[]{:S(2)}, u32[]{:S(2)}) collective-permute-start(f32[136,128]{1,0:T(8,128)S(1)} %add_add_fusion.keep), channel_id=1, source_target_pairs={{0,32},{32,0},{64,96},{96,64},{1,33},{33,1},{65,97},{97,65},{2,34}... | collective-permute-start | bytes 208904 | tf_op jit(solution)/shard_map/ppermute | solution.py:591
  (2 other events, 28.2 us)
